TPU v7x, 32 devices: a whole 2x2x4 slice. The times are simulated.
32 devices in a mesh: groups: 2 (over x), fsdp: 2 (over core), rows: 8 (over z, y).
Axes of the slice: x: 2, y: 2, z: 4, core: 2. Of those that a mesh axis runs over, the one named last changes fastest.
Arguments:
- tokens: bfloat16 [4, 128, 16, 1024], P(('groups', 'fsdp'), 'rows'), parts along dimension 0, may hold values from -6 to 6
- cell_mask: int32 [4, 128, 16], P(('groups', 'fsdp'), 'rows'), parts along dimension 0, may hold values 0 or 1
- shifts: int32 [2], replicated, may hold values from 1 to 15
- projection_in: bfloat16 [1024, 1536], P(('fsdp', 'rows')), may hold values from -2 to 2
- projection_out: bfloat16 [512, 1024], P(('fsdp', 'rows')), may hold values from -0.25 to 0.25
- cotangent: bfloat16 [4, 128, 16, 1024], P(('groups', 'fsdp'), 'rows'), parts along dimension 0, may hold values from -6 to 6
Outputs:
- output: bfloat16 [4, 128, 16, 1024], P(('groups', 'fsdp'), 'rows'), parts along dimension 0
- grad_tokens: bfloat16 [4, 128, 16, 1024], P(('groups', 'fsdp'), 'rows'), parts along dimension 0
- projection_in_grad: float32 [2048, 1536], P(('groups', 'fsdp', 'rows')), parts along dimension 0
- projection_out_grad: float32 [1024, 1024], P(('groups', 'fsdp', 'rows')), parts along dimension 0
There are 2 independent parts, one for each index of `groups`. A program takes and returns all parts, laid end to end along the dimension named above; an argument that names none is the same for every part. Nothing has to cross between parts.
All inputs are finite; a program needn't handle non-finite values. No bound on the sum of `cell_mask` on one device may be relied on, other than what follows from the above.
Results may differ from a plain program's by a relative error of at most 0.011.
Values may be sent and summed in bfloat16 or wider, within the bound.
No kernel may reach another device: no remote copies, remote signals or barrier semaphores. Data moves between devices by JAX's collectives and lax.ppermute only.
A program may use at most 64 MiB of HBM per device.

v0:
```python
import functools

import jax
import jax.numpy as jnp
import numpy as np
from jax import lax
from jax.experimental import pallas as pl
from jax.experimental.pallas import tpu as pltpu
from jax.sharding import PartitionSpec as P

HEADS = 8
HD = 64
PAIR = 2 * HD
F32 = jnp.float32
BF16 = jnp.bfloat16
VM = pl.BlockSpec(memory_space=pltpu.VMEM)
SM = pl.BlockSpec(memory_space=pltpu.SMEM)


def stage_masks(rows):
    bits = [1 << b for b in range(rows.bit_length() - 1)]
    far = bits[:1:-1]
    return (far + bits[:2], far + bits[:2][::-1])


def slot_masks(rows, core):
    masks = [0]
    for m in stage_masks(rows)[core]:
        masks = masks + [a ^ m for a in masks]
    return np.array(masks, np.int32)


def exchange(block, rows, stage):
    masks = stage_masks(rows)
    pairs = [
        (c * rows + i, c * rows + (i ^ masks[c][stage])) for c in range(2) for i in range(rows)
    ]
    return lax.ppermute(block, ("fsdp", "rows"), pairs)


def swap_cores(block):
    return lax.ppermute(block, "fsdp", [(0, 1), (1, 0)])


def shifted(block, rows, distance):
    return lax.ppermute(block, "rows", [((i - distance) % rows, i) for i in range(rows)])


def call(kernel, outs, specs, scratch=(), flops=0, moved=0, name=None):
    return pl.pallas_call(
        kernel,
        out_shape=tuple(jax.ShapeDtypeStruct(s, d) for s, d in outs),
        in_specs=list(specs),
        out_specs=tuple(VM for _ in outs),
        scratch_shapes=list(scratch),
        compiler_params=pltpu.CompilerParams(vmem_limit_bytes=40 << 20),
        cost_estimate=pl.CostEstimate(flops=flops, bytes_accessed=moved, transcendentals=0),
        name=name,
    )


def dot(a, b, ca=1, cb=0):
    return lax.dot_general(a, b, (((ca,), (cb,)), ((), ())), preferred_element_type=F32)


def place(full_in, full_out, piece, table, first, count):
    size = piece.shape[0] // count
    small = size // 2
    wide = full_in.shape[1]
    side = full_out.shape[1] // 2

    def step(j, carry):
        block = table[first + j]
        at = pl.multiple_of(block * size, size)
        at_out = pl.multiple_of(block * small, small)
        of = pl.multiple_of(j * size, size)
        full_in[pl.ds(at, size), :] = piece[pl.ds(of, size), pl.ds(0, wide)]
        for h in range(2):
            from_at = pl.multiple_of(of + h * small, small)
            full_out[pl.ds(at_out, small), pl.ds(h * side, side)] = piece[
                pl.ds(from_at, small), pl.ds(wide, side)
            ]
        return carry

    lax.fori_loop(0, count, step, 0)


def pick(dst, src, table, count, size):
    def step(j, carry):
        at = pl.multiple_of(table[j] * size, size)
        dst[pl.ds(pl.multiple_of(j * size, size), size), :] = src[pl.ds(at, size), :]
        return carry

    lax.fori_loop(0, count, step, 0)


def borrowed_rows(scal, low, count, cols, forward):
    row = (lax.broadcasted_iota(jnp.int32, (count, 1), 0) + low) // cols
    return row < scal[0] if forward else row >= scal[0]


def norm_kernel(scal, table, own, halo, xw, normed_bf, ordered, mean_out, inv_out, turned, *, low, cols, forward, blocks):
    half = own.shape[0] // 2
    take = borrowed_rows(scal, low, half, cols, forward)
    keep_low = half - low
    xw[pl.ds(keep_low, half), :] = own[pl.ds(keep_low, half), :]
    mixed = jnp.where(take, halo[pl.ds(0, half), :].astype(F32), own[pl.ds(low, half), :].astype(F32))
    xw[pl.ds(low, half), :] = mixed.astype(BF16)
    x = xw[...].astype(F32)
    mean = jnp.mean(x, axis=-1, keepdims=True)
    centered = x - mean
    inv = lax.rsqrt(jnp.mean(centered * centered, axis=-1, keepdims=True) + 1e-05)
    normed = centered * inv
    normed_bf[...] = normed.astype(BF16)
    mean_out[...] = mean
    inv_out[...] = inv
    turned[...] = normed.T.astype(BF16)
    pick(ordered, turned, table, blocks, turned.shape[0] // blocks)


def forward_kernel(place_at, order, normed_bf, bias, *refs, blocks):
    pieces, (full, full_out, packed, attn, ctx, ctx_ordered, turned) = refs[:-7], refs[-7:]
    each = blocks // len(pieces)
    for i, w in enumerate(pieces):
        place(full, full_out, w, place_at, i * each, each)
    hidden = ctx.shape[1]
    packed[...] = dot(normed_bf[...], full[...]).astype(BF16)
    cells = normed_bf.shape[0]
    first = lax.broadcasted_iota(jnp.int32, (cells, PAIR), 1) < HD
    for p in range(HEADS // 2):
        lanes = pl.ds(p * PAIR, PAIR)
        q = packed[:, lanes].astype(F32)
        k = packed[:, pl.ds(hidden + p * PAIR, PAIR)]
        v = packed[:, pl.ds(2 * hidden + p * PAIR, PAIR)]
        parts = []
        for side in range(2):
            q_one = jnp.where(first if side == 0 else ~first, q, 0.0).astype(BF16)
            scores = dot(q_one, k, 1, 1) * (HD ** (-0.5)) + bias[...]
            e = jnp.exp(scores - jnp.max(scores, axis=-1, keepdims=True))
            a = e * (1.0 / jnp.sum(e, axis=-1, keepdims=True))
            attn[2 * p + side] = a
            parts.append(dot(a.astype(BF16), v))
        both = jnp.where(first, parts[0], parts[1])
        ctx[:, lanes] = both.astype(BF16)
        turned[lanes, :] = both.T.astype(BF16)
    pick(ctx_ordered, turned, order, blocks, turned.shape[0] // blocks)


def term_out_kernel(scal, ctx_ordered, own, halo, cot, keep, send, *, low, cols, forward):
    half = halo.shape[0]
    take = borrowed_rows(scal, low, half, cols, forward)
    keep_low = half - low
    cot[pl.ds(keep_low, half), :] = own[pl.ds(keep_low, half), :]
    cot[pl.ds(low, half), :] = jnp.where(
        take, halo[...].astype(F32), own[pl.ds(low, half), :].astype(F32)
    ).astype(BF16)
    n = keep.shape[0]
    send[...] = dot(ctx_ordered[pl.ds(n, n), :], cot[...]).astype(BF16)
    keep[...] = dot(ctx_ordered[pl.ds(0, n), :], cot[...])


def half_backward(packed, attn, gctx, gp, first_pair, pairs):
    cells = packed.shape[0]
    hidden = packed.shape[1] // 3
    width = pairs * PAIR
    first = lax.broadcasted_iota(jnp.int32, (cells, PAIR), 1) < HD
    for i in range(pairs):
        p = first_pair + i
        q = packed[:, pl.ds(p * PAIR, PAIR)]
        k = packed[:, pl.ds(hidden + p * PAIR, PAIR)]
        v = packed[:, pl.ds(2 * hidden + p * PAIR, PAIR)]
        g = gctx[:, pl.ds(p * PAIR, PAIR)]
        gf = g.astype(F32)
        gq, gk, gv = [], [], []
        for side in range(2):
            g_one = jnp.where(first if side == 0 else ~first, gf, 0.0).astype(BF16)
            a = attn[2 * p + side]
            ga = dot(g_one, v, 1, 1)
            inner = jnp.sum(ga * a, axis=-1, keepdims=True)
            gs = (a * (ga - inner) * (HD ** (-0.5))).astype(BF16)
            gq.append(dot(gs, k))
            gk.append(dot(gs, q, 0, 0))
            gv.append(dot(a.astype(BF16), g, 0, 0))
        for t, two in enumerate((gq, gk, gv)):
            gp[:, pl.ds(t * width + i * PAIR, PAIR)] = jnp.where(first, two[0], two[1]).astype(BF16)


def term_of(ordered, gp, keep, send):
    n = keep.shape[0]
    send[...] = dot(ordered[pl.ds(n, n), :], gp[...]).astype(BF16)
    keep[...] = dot(ordered[pl.ds(0, n), :], gp[...])


def backward_a_kernel(cot, packed, attn, ordered, full, gctx, gp, keep, send):
    gctx[...] = dot(cot[...], full[...], 1, 1).astype(BF16)
    half_backward(packed, attn, gctx, gp, 0, HEADS // 4)
    term_of(ordered, gp, keep, send)


def backward_b_kernel(packed, attn, gctx, ordered, gp, keep, send):
    half_backward(packed, attn, gctx, gp, HEADS // 4, HEADS // 4)
    term_of(ordered, gp, keep, send)


def grad_kernel(xw, mean, inv, gp_a, gp_b, full, cot, grad, gp):
    width = gp.shape[1] // 6
    for t in range(3):
        gp[:, pl.ds(2 * t * width, width)] = gp_a[:, pl.ds(t * width, width)]
        gp[:, pl.ds((2 * t + 1) * width, width)] = gp_b[:, pl.ds(t * width, width)]
    gn = dot(gp[...], full[...], 1, 1)
    normed = (xw[...].astype(F32) - mean[...]) * inv[...]
    m1 = jnp.mean(gn, axis=-1, keepdims=True)
    m2 = jnp.mean(gn * normed, axis=-1, keepdims=True)
    grad[...] = (cot[...].astype(F32) + inv[...] * (gn - m1 - normed * m2)).astype(BF16)


def output_kernel(scal, own, ctx, back, full, out, mixed, *, low, cols, forward):
    half = back.shape[0]
    take = borrowed_rows(scal, low, half, cols, forward)
    keep_low = half - low
    mixed[pl.ds(keep_low, half), :] = ctx[pl.ds(keep_low, half), :]
    mixed[pl.ds(low, half), :] = jnp.where(
        take, back[...].astype(F32), ctx[pl.ds(low, half), :].astype(F32)
    ).astype(BF16)
    out[...] = (own[...].astype(F32) + dot(mixed[...], full[...])).astype(BF16)


def after(value, *done):
    return lax.optimization_barrier((value, *done))[0]


def gather_pieces(shard, rows, halo):
    stages = len(stage_masks(rows)[0])
    own = shard
    for stage in range(stages - 3):
        own = jnp.concatenate([own, exchange(own, rows, stage)], axis=0)
    a, b, c = stages - 3, stages - 2, stages - 1
    got_a = exchange(own, rows, a)
    got_b = exchange(own, rows, b)
    got_c = exchange(own, rows, c)
    got_ab = exchange(after(got_a, got_b, halo), rows, b)
    got_ac = exchange(after(got_a, got_c), rows, c)
    got_bc = exchange(after(got_b, got_c), rows, c)
    got_abc = exchange(after(got_ab, got_ac), rows, c)
    held = (own, got_a, got_b, got_ab, got_c, got_ac, got_bc, got_abc)
    return held + tuple(swap_cores(x) for x in held)


def scatter_from(keep, arrived, rows):
    n = len(stage_masks(rows)[0])
    q = keep.shape[0] // 4
    keep = keep + arrived.astype(F32)
    first = keep[2 * q :].astype(BF16)
    h = 2 * q
    far = exchange(keep[h:].astype(BF16), rows, n - 1)
    keep = keep[:h] + far.astype(F32)
    near = second = exchange(keep[q:].astype(BF16), rows, n - 2)
    keep = keep[:q] + second.astype(F32)
    for stage in range(n - 3, -1, -1):
        half = keep.shape[0] // 2
        arrived = exchange(keep[half:].astype(BF16), rows, stage)
        if stage:
            keep = keep[:half] + arrived.astype(F32)
    return keep[: keep.shape[0] // 2], arrived, first, (far, near, second)


def finish_kernel(keep_a, last_a, keep_b, last_b, out):
    fine = keep_a.shape[1] // 3
    for i, (keep, last) in enumerate(((keep_a, last_a), (keep_b, last_b))):
        for t in range(3):
            cols = pl.ds(t * fine, fine)
            out[:, pl.ds((2 * t + i) * fine, fine)] = keep[:, cols] + last[:, cols].astype(F32)


def branch(tokens, cell_mask, shifts, projection_in, projection_out, cotangent, *, forward):
    rows = lax.axis_size("rows")
    row_count, cols, dim = tokens.shape[1:]
    cells = row_count * cols
    half = cells // 2
    hidden = HEADS * HD
    low = 0 if forward else half
    distance = -1 if forward else 1
    core = lax.axis_index("fsdp")
    me = lax.axis_index("rows")
    blocks = 2 * rows
    m0 = jnp.asarray(slot_masks(rows, 0))
    m1 = jnp.asarray(slot_masks(rows, 1))
    mine = jnp.where(core == 0, m0, m1) ^ me
    theirs = jnp.where(core == 0, m1, m0) ^ me
    table = jnp.concatenate([core * rows + mine, (1 - core) * rows + theirs]).astype(jnp.int32)
    scal = shifts.astype(jnp.int32)
    s_row, s_col = scal[0], scal[1]
    part = lambda a: lax.slice_in_dim(a, low, low + half, axis=0)

    own = tokens.reshape(cells, dim)
    own_cot = cotangent.reshape(cells, dim)
    own_mask = cell_mask.astype(BF16).reshape(cells, 1)
    tile = 16
    mask_rows = jnp.pad(part(own_mask).T, ((0, tile - 1), (0, dim - half)))
    halo = shifted(jnp.concatenate([part(own), mask_rows], axis=0), rows, distance)
    flat_out = jnp.concatenate([projection_out[:, : dim // 2], projection_out[:, dim // 2 :]], axis=0)
    both = jnp.concatenate([projection_in, flat_out], axis=1)
    in_parts = gather_pieces(both, rows, halo)
    halo_cot = shifted(after(part(own_cot), in_parts[5], in_parts[6]), rows, distance)
    halo_mask = halo[half, :half][:, None]

    cell = jnp.arange(cells, dtype=jnp.int32)
    cell_row, cell_col = cell // cols, cell % cols
    from_other = (cell_row < s_row) if forward else (cell_row >= s_row)
    pad = ((low, half - low), (0, 0))
    key_ok = jnp.where(from_other, jnp.pad(halo_mask, pad)[:, 0], own_mask[:, 0]) > 0
    at_wrap = me == (rows - 1 if forward else 0)
    region = 2 * ((cell_row < s_row) & at_wrap).astype(jnp.int32) + (cell_col < s_col).astype(
        jnp.int32
    )
    allowed = (region[:, None] == region[None, :]) & (
        key_ok[None, :] | (cell[:, None] == cell[None, :])
    )
    bias = jnp.where(allowed, 0.0, -1e30).astype(F32)

    shape_kw = dict(low=low, cols=cols, forward=forward)
    xw, normed_bf, ordered, mean, inv = call(
        functools.partial(norm_kernel, blocks=blocks, **shape_kw),
        [((cells, dim), BF16), ((cells, dim), BF16), ((dim, cells), BF16), ((cells, 1), F32), ((cells, 1), F32)],
        [SM, SM, VM, VM],
        [pltpu.VMEM((dim, cells), BF16)],
        flops=20 * cells * dim,
        moved=10 * cells * dim,
        name="norm",
    )(scal, table, own, halo)
    full_in, full_out, packed, attn, ctx, ctx_ordered = call(
        functools.partial(forward_kernel, blocks=blocks),
        [((dim, 3 * hidden), BF16), ((hidden, dim), BF16), ((cells, 3 * hidden), BF16), ((HEADS, cells, cells), F32), ((cells, hidden), BF16), ((hidden, cells), BF16)],
        [SM, SM, VM, VM] + [VM] * len(in_parts),
        [pltpu.VMEM((hidden, cells), BF16)],
        flops=6 * cells * dim * 3 * hidden,
        moved=10 << 20,
        name="fwd",
    )(table, table, normed_bf, bias, *in_parts)
    back_ctx = shifted(part(ctx), rows, -distance)
    cot, keep_out, send_out = call(
        functools.partial(term_out_kernel, **shape_kw),
        [((cells, dim), BF16), ((hidden // 2, dim), F32), ((hidden // 2, dim), BF16)],
        [SM, VM, VM, VM],
        flops=2 * cells * dim * hidden,
        moved=4 << 20,
        name="term_out",
    )(scal, ctx_ordered, own_cot, halo_cot)
    swapped_out = swap_cores(send_out)
    quart = 3 * hidden // 2
    half_outs = [((cells, quart), BF16), ((dim // 2, quart), F32), ((dim // 2, quart), BF16)]
    gctx, gp_a, keep_a, send_a = call(
        backward_a_kernel,
        [((cells, hidden), BF16)] + half_outs,
        [VM] * 5,
        flops=4 * cells * dim * 3 * hidden,
        moved=6 << 20,
        name="bwd_a",
    )(cot, packed, attn, ordered, full_out)
    swapped_a = swap_cores(send_a)
    gp_b, keep_b, send_b = call(
        backward_b_kernel,
        half_outs,
        [VM, VM, VM, VM],
        flops=4 * cells * dim * 3 * hidden,
        moved=6 << 20,
        name="bwd_b",
    )(packed, attn, after(gctx, swapped_out, back_ctx), ordered)
    swapped_b = swap_cores(send_b)
    kept_out, last_out, _, _ = scatter_from(keep_out, swapped_out, rows)
    grad_out = kept_out + last_out.astype(F32)
    kept_a, last_a, first_a, seen_a = scatter_from(keep_a, swapped_a, rows)
    kept_b, last_b, _, _ = scatter_from(keep_b, swapped_b, rows)
    (grad_in,) = call(
        finish_kernel,
        [((dim // blocks, 3 * hidden), F32)],
        [VM] * 4,
        moved=1 << 20,
        name="finish",
    )(kept_a, last_a, kept_b, last_b)
    (grad_win,) = call(
        grad_kernel,
        [((cells, dim), BF16)],
        [VM] * 7,
        [pltpu.VMEM((cells, 3 * hidden), BF16)],
        flops=2 * cells * dim * 3 * hidden,
        moved=6 << 20,
        name="grad",
    )(xw, mean, inv, gp_a, after(gp_b, first_a), full_in, cot)
    back_grad = shifted(part(grad_win), rows, -distance)
    (output,) = call(
        functools.partial(output_kernel, **shape_kw),
        [((cells, dim), BF16)],
        [SM, VM, VM, VM, VM],
        [pltpu.VMEM((cells, hidden), BF16)],
        flops=2 * cells * dim * hidden,
        moved=3 << 20,
        name="output",
    )(scal, own, ctx, after(back_ctx, seen_a[0]), full_out)
    own_grad = jnp.where(from_other[:, None], jnp.pad(back_grad, pad), grad_win)
    shape = tokens.shape
    return (output.reshape(shape), own_grad.reshape(shape), grad_in, grad_out)


def body(tokens, cell_mask, shifts, projection_in, projection_out, cotangent):
    return lax.cond(
        shifts[0] <= tokens.shape[1] // 2,
        functools.partial(branch, forward=True),
        functools.partial(branch, forward=False),
        tokens, cell_mask, shifts, projection_in, projection_out, cotangent,
    )


def solution(mesh):
    placed = (
        P(("groups", "fsdp"), "rows", None, None),
        P(("groups", "fsdp"), "rows", None),
        P(),
        P(("fsdp", "rows"), None),
        P(("fsdp", "rows"), None),
        P(("groups", "fsdp"), "rows", None, None),
    )
    return jax.shard_map(
        body,
        mesh=mesh,
        in_specs=placed,
        out_specs=(
            P(("groups", "fsdp"), "rows", None, None),
            P(("groups", "fsdp"), "rows", None, None),
            P(("groups", "fsdp", "rows"), None),
            P(("groups", "fsdp", "rows"), None),
        ),
        check_vma=False,
    )
```

profile of v0, /device:TPU:0, one launch (start us, length us, event | category | flops | bytes accessed | tf_op | source)
XLA Modules:
  0.0 101.4 jit_solution(5432801617798849192)
XLA Ops:
  1.3 100.2 %conditional.1 = (bf16[1,16,16,1024]{3,2,1,0:T(8,128)(2,1)}, bf16[1,16,16,1024]{3,2,1,0:T(8,128)(2,1)}, f32[64,1536]{1,0:T(8,128)}, f32[32,1024]{1,0:T(8,128)}) conditional(s32[]{:T(128)} %bitcast.18, (bf16[1,16,16,1024]{3,2,1,0:T(8,128)(2,1)}, s32[8]{0:T(128)}, s32[8]{0:T(128)}, s32[1,16,16]{2,1,0:T(8,128)}, s32[2]{0:T(128)}, ...), branch_computations={%region_0.1_spmd, %region_1.2_spmd} | conditional | flops 6990571520 | bytes 107588672 | solution.py:406
  3.3 6.1 %collective-permute-start.31 = (bf16[144,1024]{1,0:T(8,128)(2,1)S(1)}, bf16[144,1024]{1,0:T(8,128)(2,1)S(1)}, u32[]{:S(2)}, u32[]{:S(2)}) collective-permute-start(bf16[144,1024]{1,0:T(8,128)(2,1)S(1)} %fusion.13), channel_id=1, source_target_pairs={{1,0},{2,1},{3,2},{4,3},{5,4},{6,5},{7,6},{0,7},{9,8},{10,9},{11,1... | collective-permute-start | bytes 884744 | tf_op jit(solution)/shard_map/cond/branch_1_fun/ppermute | solution.py:46
  11.2 1.0 collective-permute-start.32
  12.8 13.0 %collective-permute-done.35.refs_4_ = bf16[64,2048]{1,0:T(8,128)(2,1)S(1)} collective-permute-done((bf16[64,2048]{1,0:T(8,128)(2,1)S(1)}, bf16[64,2048]{1,0:T(8,128)(2,1)S(1)}, u32[]{:S(2)}, u32[]{:S(2)}) %collective-permute-start.35) | collective-permute-done | bytes 262176 | tf_op jit(solution)/shard_map/cond/branch_1_fun/ppermute | solution.py:38
  25.8 1.3 %collective-permute-done.32.refs_1_ = bf16[64,2048]{1,0:T(8,128)(2,1)S(1)} collective-permute-done((bf16[64,2048]{1,0:T(8,128)(2,1)S(1)}, bf16[64,2048]{1,0:T(8,128)(2,1)S(1)}, u32[]{:S(2)}, u32[]{:S(2)}) %collective-permute-start.32) | collective-permute-done | bytes 262176 | tf_op jit(solution)/shard_map/cond/branch_1_fun/ppermute | solution.py:38
  27.0 1.4 %collective-permute-start.36 = (bf16[64,2048]{1,0:T(8,128)(2,1)S(1)}, bf16[64,2048]{1,0:T(8,128)(2,1)S(1)}, u32[]{:S(2)}, u32[]{:S(2)}) collective-permute-start(bf16[64,2048]{1,0:T(8,128)(2,1)S(1)} %collective-permute-done.32.refs_1_), channel_id=1, source_target_pairs={{0,2},{1,3},{2,0},{3,1},{4,6},{5,7},{6,4},{7,5},{8,9},{9,8},{10,11... | collective-permute-start | bytes 786440 | tf_op jit(solution)/shard_map/cond/branch_1_fun/ppermute | solution.py:38
  29.0 1.3 %fusion.19 = s32[256]{0:T(256)S(1)} fusion(pred[]{:T(512)S(6)} %eq.45, s32[]{:T(128)} %bitcast.12, s32[]{:T(128)} %bitcast.11), kind=kLoop, calls=%fused_computation.86 | loop fusion | flops 4608 | bytes 1033 | tf_op jit(solution)/shard_map/cond/branch_1_fun/add | solution.py:313
  31.1 3.9 %collective-permute-done.36.refs_5_ = bf16[64,2048]{1,0:T(8,128)(2,1)S(1)} collective-permute-done((bf16[64,2048]{1,0:T(8,128)(2,1)S(1)}, bf16[64,2048]{1,0:T(8,128)(2,1)S(1)}, u32[]{:S(2)}, u32[]{:S(2)}) %collective-permute-start.36) | collective-permute-done | bytes 262176 | tf_op jit(solution)/shard_map/cond/branch_1_fun/ppermute | solution.py:38
  34.9 1.9 %collective-permute-done.34.refs_3_ = bf16[64,2048]{1,0:T(8,128)(2,1)S(1)} collective-permute-done((bf16[64,2048]{1,0:T(8,128)(2,1)S(1)}, bf16[64,2048]{1,0:T(8,128)(2,1)S(1)}, u32[]{:S(2)}, u32[]{:S(2)}) %collective-permute-start.34) | collective-permute-done | bytes 262176 | tf_op jit(solution)/shard_map/cond/branch_1_fun/ppermute | solution.py:38
  36.8 1.0 %collective-permute-start.38 = (bf16[64,2048]{1,0:T(8,128)(2,1)S(1)}, bf16[64,2048]{1,0:T(8,128)(2,1)S(1)}, u32[]{:S(2)}, u32[]{:S(2)}) collective-permute-start(bf16[64,2048]{1,0:T(8,128)(2,1)S(1)} %collective-permute-done.34.refs_3_), channel_id=1, source_target_pairs={{0,2},{1,3},{2,0},{3,1},{4,6},{5,7},{6,4},{7,5},{8,9},{9,8},{10,11... | collective-permute-start | bytes 786440 | tf_op jit(solution)/shard_map/cond/branch_1_fun/ppermute | solution.py:38
  40.2 3.0 %collective-permute-done.38.refs_7_ = bf16[64,2048]{1,0:T(8,128)(2,1)S(1)} collective-permute-done((bf16[64,2048]{1,0:T(8,128)(2,1)S(1)}, bf16[64,2048]{1,0:T(8,128)(2,1)S(1)}, u32[]{:S(2)}, u32[]{:S(2)}) %collective-permute-start.38) | collective-permute-done | bytes 262176 | tf_op jit(solution)/shard_map/cond/branch_1_fun/ppermute | solution.py:38
  43.9 3.3 %collective-permute-start.48 = (bf16[128,1024]{1,0:T(8,128)(2,1)S(1)}, bf16[128,1024]{1,0:T(8,128)(2,1)S(1)}, u32[]{:S(2)}, u32[]{:S(2)}) collective-permute-start(bf16[128,1024]{1,0:T(8,128)(2,1)S(1)} %bitcast.35), channel_id=1, source_target_pairs={{1,0},{2,1},{3,2},{4,3},{5,4},{6,5},{7,6},{0,7},{9,8},{10,9},{11,1... | collective-permute-start | bytes 786440 | tf_op jit(solution)/shard_map/cond/branch_1_fun/ppermute | solution.py:46
  47.3 1.7 %norm.3 = (bf16[256,1024]{1,0:T(8,128)(2,1)S(1)}, bf16[256,1024]{1,0:T(8,128)(2,1)S(1)}, bf16[1024,256]{1,0:T(8,128)(2,1)S(1)}, f32[256,1]{1,0:T(8,128)S(1)}, f32[256,1]{1,0:T(8,128)S(1)}) custom-call(s32[2]{0:T(128)S(1)} %copy-done.5, s32[16]{0:T(128)S(1)} %pad_add_fusion.1.table.place_at.order, bf16[256,1024]{1,0:T(8,128)(2,1)} %bitcast.24, ...), custom_call_target="tpu_custom_call" | custom-call | flops 5242880 | bytes 2621440 | tf_op jit(solution)/shard_map/cond/branch_1_fun/norm/pallas_call | solution.py:322
  49.0 3.2 %fwd.3 = (bf16[1024,1536]{1,0:T(8,128)(2,1)S(1)}, bf16[512,1024]{1,0:T(8,128)(2,1)S(1)}, bf16[256,1536]{1,0:T(8,128)(2,1)S(1)}, f32[8,256,256]{2,1,0:T(8,128)S(1...) custom-call(s32[16]{0:T(128)S(1)} %pad_add_fusion.1.table.place_at.order, ...), custom_call_target="tpu_custom_call" | custom-call | flops 2415919104 | bytes 10485760 | tf_op jit(solution)/shard_map/cond/branch_1_fun/fwd/pallas_call | solution.py:331
  52.3 1.1 %collective-permute-done.48.halo = bf16[128,1024]{1,0:T(8,128)(2,1)S(1)} collective-permute-done((bf16[128,1024]{1,0:T(8,128)(2,1)S(1)}, bf16[128,1024]{1,0:T(8,128)(2,1)S(1)}, u32[]{:S(2)}, u32[]{:S(2)}) %collective-permute-start.48) | collective-permute-done | bytes 262176 | tf_op jit(solution)/shard_map/cond/branch_1_fun/ppermute | solution.py:46
  53.4 1.0 term_out.3
  54.6 2.6 %bwd_a.3 = (bf16[256,512]{1,0:T(8,128)(2,1)S(1)}, bf16[256,768]{1,0:T(8,128)(2,1)S(1)}, f32[512,768]{1,0:T(8,128)S(1)}, bf16[512,768]{1,0:T(8,128)(2,1)S(1)}) custom-call(bf16[256,1024]{1,0:T(8,128)(2,1)S(1)} %get-tuple-element.85.cot, bf16[256,1536]{1,0:T(8,128)(2,1)S(1)} %get-tuple-element.86.packed, f32[8,256,256]{2,1,0:T(8,128)S(1)} %get-tuple-element.87.attn, ...), custom_call_target="tpu_custom_call" | custom-call | flops 1610612736 | bytes 6291456 | tf_op jit(solution)/shard_map/cond/branch_1_fun/bwd_a/pallas_call | solution.py:352
  58.0 2.6 %collective-permute-start.59 = (bf16[128,1024]{1,0:T(8,128)(2,1)S(1)}, bf16[128,1024]{1,0:T(8,128)(2,1)S(1)}, u32[]{:S(2)}, u32[]{:S(2)}) collective-permute-start(bf16[128,1024]{1,0:T(8,128)(2,1)S(1)} %slice.293), channel_id=1, source_target_pairs={{0,2},{1,3},{2,0},{3,1},{4,6},{5,7},{6,4},{7,5},{8,9},{9,8},{10,11... | collective-permute-start | bytes 786440 | tf_op jit(solution)/shard_map/cond/branch_1_fun/ppermute | solution.py:38
  61.2 2.8 %collective-permute-done.47.back = bf16[128,512]{1,0:T(8,128)(2,1)S(1)} collective-permute-done((bf16[128,512]{1,0:T(8,128)(2,1)S(1)}, bf16[128,512]{1,0:T(8,128)(2,1)S(1)}, u32[]{:S(2)}, u32[]{:S(2)}) %collective-permute-start.47) | collective-permute-done | bytes 131104 | tf_op jit(solution)/shard_map/cond/branch_1_fun/ppermute | solution.py:46
  64.1 2.2 %bwd_b.3 = (bf16[256,768]{1,0:T(8,128)(2,1)S(1)}, f32[512,768]{1,0:T(8,128)S(1)}, bf16[512,768]{1,0:T(8,128)(2,1)S(1)}) custom-call(bf16[256,1536]{1,0:T(8,128)(2,1)S(1)} %get-tuple-element.86.packed, f32[8,256,256]{2,1,0:T(8,128)S(1)} %get-tuple-element.87.attn, bf16[256,512]{1,0:T(8,128)(2,1)S(1)} %get-tuple-element.99.gctx, ...), custom_call_target="tpu_custom_call" | custom-call | flops 1610612736 | bytes 6291456 | tf_op jit(solution)/shard_map/cond/branch_1_fun/bwd_b/pallas_call | solution.py:361
  66.5 1.0 collective-permute-start.60
  67.7 1.4 %collective-permute-start.50 = (bf16[256,768]{1,0:T(8,128)(2,1)S(1)}, bf16[256,768]{1,0:T(8,128)(2,1)S(1)}, u32[]{:S(2)}, u32[]{:S(2)}) collective-permute-start(bf16[256,768]{1,0:T(8,128)(2,1)S(1)} %slice.292), channel_id=1, source_target_pairs={{0,2},{1,3},{2,0},{3,1},{4,6},{5,7},{6,4},{7,5},{8,9},{9,8},{10,11... | collective-permute-start | bytes 1179656 | tf_op jit(solution)/shard_map/cond/branch_1_fun/ppermute | solution.py:38
  69.1 1.3 %grad.3 = bf16[256,1024]{1,0:T(8,128)(2,1)S(1)} custom-call(bf16[256,1024]{1,0:T(8,128)(2,1)S(1)} %get-tuple-element.93.xw, f32[256,1]{1,0:T(8,128)S(1)} %get-tuple-element.94.mean, f32[256,1]{1,0:T(8,128)S(1)} %get-tuple-element.95.inv, bf16[256,768]{1,0:T(8,128)(2,1)S(1)} %get-tuple-element.96.gp_a, bf16[256,768]{1,0:T(8,128)(2,1)S(1)} %get-tuple-element.101.gp_b, ...), custom_call_target="tpu_custom_call" | custom-call | flops 805306368 | bytes 6291456 | tf_op jit(solution)/shard_map/cond/branch_1_fun/grad/pallas_call | solution.py:381
  70.8 2.1 %collective-permute-done.60 = bf16[64,1024]{1,0:T(8,128)(2,1)S(1)} collective-permute-done((bf16[64,1024]{1,0:T(8,128)(2,1)S(1)}, bf16[64,1024]{1,0:T(8,128)(2,1)S(1)}, u32[]{:S(2)}, u32[]{:S(2)}) %collective-permute-start.60) | collective-permute-done | bytes 131104 | tf_op jit(solution)/shard_map/cond/branch_1_fun/ppermute | solution.py:38
  72.9 1.7 %collective-permute-start.61 = (bf16[32,1024]{1,0:T(8,128)(2,1)S(1)}, bf16[32,1024]{1,0:T(8,128)(2,1)S(1)}, u32[]{:S(2)}, u32[]{:S(2)}) collective-permute-start(bf16[32,1024]{1,0:T(8,128)(2,1)S(1)} %slice.299), channel_id=1, source_target_pairs={{0,4},{1,5},{2,6},{3,7},{4,0},{5,1},{6,2},{7,3},{8,12},{9,13},{10,... | collective-permute-start | bytes 196616 | tf_op jit(solution)/shard_map/cond/branch_1_fun/ppermute | solution.py:38
  74.9 4.4 %collective-permute-start.56 = (bf16[256,768]{1,0:T(8,128)(2,1)S(1)}, bf16[256,768]{1,0:T(8,128)(2,1)S(1)}, u32[]{:S(2)}, u32[]{:S(2)}) collective-permute-start(bf16[256,768]{1,0:T(8,128)(2,1)S(1)} %slice.291), channel_id=1, source_target_pairs={{0,2},{1,3},{2,0},{3,1},{4,6},{5,7},{6,4},{7,5},{8,9},{9,8},{10,11... | collective-permute-start | bytes 1179656 | tf_op jit(solution)/shard_map/cond/branch_1_fun/ppermute | solution.py:38
  80.0 2.5 %collective-permute-start.53 = (bf16[128,768]{1,0:T(8,128)(2,1)S(1)}, bf16[128,768]{1,0:T(8,128)(2,1)S(1)}, u32[]{:S(2)}, u32[]{:S(2)}) collective-permute-start(bf16[128,768]{1,0:T(8,128)(2,1)S(1)} %slice.295), channel_id=1, source_target_pairs={{0,1},{1,0},{2,3},{3,2},{4,5},{5,4},{6,7},{7,6},{8,10},{9,11},{10,... | collective-permute-start | bytes 589832 | tf_op jit(solution)/shard_map/cond/branch_1_fun/ppermute | solution.py:38
  82.6 3.2 %collective-permute-done.56 = bf16[256,768]{1,0:T(8,128)(2,1)S(1)} collective-permute-done((bf16[256,768]{1,0:T(8,128)(2,1)S(1)}, bf16[256,768]{1,0:T(8,128)(2,1)S(1)}, u32[]{:S(2)}, u32[]{:S(2)}) %collective-permute-start.56) | collective-permute-done | bytes 393248 | tf_op jit(solution)/shard_map/cond/branch_1_fun/ppermute | solution.py:38
  85.9 4.8 %collective-permute-start.57 = (bf16[128,768]{1,0:T(8,128)(2,1)S(1)}, bf16[128,768]{1,0:T(8,128)(2,1)S(1)}, u32[]{:S(2)}, u32[]{:S(2)}) collective-permute-start(bf16[128,768]{1,0:T(8,128)(2,1)S(1)} %slice.294), channel_id=1, source_target_pairs={{0,1},{1,0},{2,3},{3,2},{4,5},{5,4},{6,7},{7,6},{8,10},{9,11},{10,... | collective-permute-start | bytes 589832 | tf_op jit(solution)/shard_map/cond/branch_1_fun/ppermute | solution.py:38
  90.7 3.5 %collective-permute-start.54 = (bf16[64,768]{1,0:T(8,128)(2,1)S(1)}, bf16[64,768]{1,0:T(8,128)(2,1)S(1)}, u32[]{:S(2)}, u32[]{:S(2)}) collective-permute-start(bf16[64,768]{1,0:T(8,128)(2,1)S(1)} %slice.298), channel_id=1, source_target_pairs={{0,4},{1,5},{2,6},{3,7},{4,0},{5,1},{6,2},{7,3},{8,12},{9,13},{10,... | collective-permute-start | bytes 294920 | tf_op jit(solution)/shard_map/cond/branch_1_fun/ppermute | solution.py:38
  94.4 3.5 %collective-permute-start.58 = (bf16[64,768]{1,0:T(8,128)(2,1)S(1)}, bf16[64,768]{1,0:T(8,128)(2,1)S(1)}, u32[]{:S(2)}, u32[]{:S(2)}) collective-permute-start(bf16[64,768]{1,0:T(8,128)(2,1)S(1)} %slice.297), channel_id=1, source_target_pairs={{0,4},{1,5},{2,6},{3,7},{4,0},{5,1},{6,2},{7,3},{8,12},{9,13},{10,... | collective-permute-start | bytes 294920 | tf_op jit(solution)/shard_map/cond/branch_1_fun/ppermute | solution.py:38
  98.8 1.8 %output.3 = bf16[256,1024]{1,0:T(8,128)(2,1)} custom-call(s32[2]{0:T(128)S(1)} %copy-done.5, bf16[256,1024]{1,0:T(8,128)(2,1)S(1)} %bitcast.25, bf16[256,512]{1,0:T(8,128)(2,1)S(1)} %get-tuple-element.81.ctx, bf16[128,512]{1,0:T(8,128)(2,1)S(1)} %collective-permute-done.47.back, bf16[512,1024]{1,0:T(8,128)(2,1)S(1)} %get-tuple-element.89.full), custom_call_target="tpu_custom_call" | custom-call | flops 268435456 | bytes 3145728 | tf_op jit(solution)/shard_map/cond/branch_1_fun/output/pallas_call | solution.py:391
  (91 shorter events, 14.0 us)
Async XLA Ops:
  1.5 26.9 %copy-start.5 = (s32[2]{0:T(128)S(1)}, s32[2]{0:T(128)}, u32[]{:S(2)}) copy-start(s32[2]{0:T(128)} %get-tuple-element.69.scal) | copy-start | bytes 28 | tf_op jit(solution)/shard_map/cond
  3.3 25.1 %collective-permute-start.31 = (bf16[144,1024]{1,0:T(8,128)(2,1)S(1)}, bf16[144,1024]{1,0:T(8,128)(2,1)S(1)}, u32[]{:S(2)}, u32[]{:S(2)}) collective-permute-start(bf16[144,1024]{1,0:T(8,128)(2,1)S(1)} %fusion.13), channel_id=1, source_target_pairs={{1,0},{2,1},{3,2},{4,3},{5,4},{6,5},{7,6},{0,7},{9,8},{10,9},{11,1... | collective-permute-start | bytes 884744 | tf_op jit(solution)/shard_map/cond/branch_1_fun/ppermute | solution.py:46
  11.1 14.7 %collective-permute-start.35 = (bf16[64,2048]{1,0:T(8,128)(2,1)S(1)}, bf16[64,2048]{1,0:T(8,128)(2,1)S(1)}, u32[]{:S(2)}, u32[]{:S(2)}) collective-permute-start(bf16[64,2048]{1,0:T(8,128)(2,1)S(1)} %maximum_maximum_fusion.1.refs_0_), channel_id=1, source_target_pairs={{0,2},{1,3},{2,0},{3,1},{4,6},{5,7},{6,4},{7,5},{8,9},{9,8},{10,11... | collective-permute-start | bytes 786440 | tf_op jit(solution)/shard_map/cond/branch_1_fun/ppermute | solution.py:38
  11.2 15.8 %collective-permute-start.32 = (bf16[64,2048]{1,0:T(8,128)(2,1)S(1)}, bf16[64,2048]{1,0:T(8,128)(2,1)S(1)}, u32[]{:S(2)}, u32[]{:S(2)}) collective-permute-start(bf16[64,2048]{1,0:T(8,128)(2,1)S(1)} %maximum_maximum_fusion.1.refs_0_), channel_id=1, source_target_pairs={{0,4},{1,5},{2,6},{3,7},{4,0},{5,1},{6,2},{7,3},{8,12},{9,13},{10,... | collective-permute-start | bytes 786440 | tf_op jit(solution)/shard_map/cond/branch_1_fun/ppermute | solution.py:38
  12.2 16.2 %collective-permute-start.33 = (bf16[64,2048]{1,0:T(8,128)(2,1)S(1)}, bf16[64,2048]{1,0:T(8,128)(2,1)S(1)}, u32[]{:S(2)}, u32[]{:S(2)}) collective-permute-start(bf16[64,2048]{1,0:T(8,128)(2,1)S(1)} %maximum_maximum_fusion.1.refs_0_), channel_id=1, source_target_pairs={{0,1},{1,0},{2,3},{3,2},{4,5},{5,4},{6,7},{7,6},{8,10},{9,11},{10,... | collective-permute-start | bytes 786440 | tf_op jit(solution)/shard_map/cond/branch_1_fun/ppermute | solution.py:38
  12.8 26.2 %collective-permute-start.39 = (bf16[64,2048]{1,0:T(8,128)(2,1)S(1)}, bf16[64,2048]{1,0:T(8,128)(2,1)S(1)}, u32[]{:S(2)}, u32[]{:S(2)}) collective-permute-start(bf16[64,2048]{1,0:T(8,128)(2,1)S(1)} %maximum_maximum_fusion.1.refs_0_), channel_id=1, source_target_pairs={{0,8},{8,0},{1,9},{9,1},{2,10},{10,2},{3,11},{11,3},{4,12},{12,4},... | collective-permute-start | bytes 786440 | tf_op jit(solution)/shard_map/cond/branch_1_fun/ppermute | solution.py:42
  27.0 7.9 %collective-permute-start.36 = (bf16[64,2048]{1,0:T(8,128)(2,1)S(1)}, bf16[64,2048]{1,0:T(8,128)(2,1)S(1)}, u32[]{:S(2)}, u32[]{:S(2)}) collective-permute-start(bf16[64,2048]{1,0:T(8,128)(2,1)S(1)} %collective-permute-done.32.refs_1_), channel_id=1, source_target_pairs={{0,2},{1,3},{2,0},{3,1},{4,6},{5,7},{6,4},{7,5},{8,9},{9,8},{10,11... | collective-permute-start | bytes 786440 | tf_op jit(solution)/shard_map/cond/branch_1_fun/ppermute | solution.py:38
  28.4 8.4 %collective-permute-start.34 = (bf16[64,2048]{1,0:T(8,128)(2,1)S(1)}, bf16[64,2048]{1,0:T(8,128)(2,1)S(1)}, u32[]{:S(2)}, u32[]{:S(2)}) collective-permute-start(bf16[64,2048]{1,0:T(8,128)(2,1)S(1)} %collective-permute-done.32.refs_1_), channel_id=1, source_target_pairs={{0,1},{1,0},{2,3},{3,2},{4,5},{5,4},{6,7},{7,6},{8,10},{9,11},{10,... | collective-permute-start | bytes 786440 | tf_op jit(solution)/shard_map/cond/branch_1_fun/ppermute | solution.py:38
  30.3 9.3 %collective-permute-start.37 = (bf16[64,2048]{1,0:T(8,128)(2,1)S(1)}, bf16[64,2048]{1,0:T(8,128)(2,1)S(1)}, u32[]{:S(2)}, u32[]{:S(2)}) collective-permute-start(bf16[64,2048]{1,0:T(8,128)(2,1)S(1)} %collective-permute-done.33.refs_2_), channel_id=1, source_target_pairs={{0,2},{1,3},{2,0},{3,1},{4,6},{5,7},{6,4},{7,5},{8,9},{9,8},{10,11... | collective-permute-start | bytes 786440 | tf_op jit(solution)/shard_map/cond/branch_1_fun/ppermute | solution.py:38
  31.1 8.1 %collective-permute-start.43 = (bf16[64,2048]{1,0:T(8,128)(2,1)S(1)}, bf16[64,2048]{1,0:T(8,128)(2,1)S(1)}, u32[]{:S(2)}, u32[]{:S(2)}) collective-permute-start(bf16[64,2048]{1,0:T(8,128)(2,1)S(1)} %collective-permute-done.35.refs_4_), channel_id=1, source_target_pairs={{0,8},{8,0},{1,9},{9,1},{2,10},{10,2},{3,11},{11,3},{4,12},{12,4},... | collective-permute-start | bytes 786440 | tf_op jit(solution)/shard_map/cond/branch_1_fun/ppermute | solution.py:42
  34.9 4.8 %collective-permute-start.41 = (bf16[64,2048]{1,0:T(8,128)(2,1)S(1)}, bf16[64,2048]{1,0:T(8,128)(2,1)S(1)}, u32[]{:S(2)}, u32[]{:S(2)}) collective-permute-start(bf16[64,2048]{1,0:T(8,128)(2,1)S(1)} %collective-permute-done.33.refs_2_), channel_id=1, source_target_pairs={{0,8},{8,0},{1,9},{9,1},{2,10},{10,2},{3,11},{11,3},{4,12},{12,4},... | collective-permute-start | bytes 786440 | tf_op jit(solution)/shard_map/cond/branch_1_fun/ppermute | solution.py:42
  36.8 6.4 %collective-permute-start.38 = (bf16[64,2048]{1,0:T(8,128)(2,1)S(1)}, bf16[64,2048]{1,0:T(8,128)(2,1)S(1)}, u32[]{:S(2)}, u32[]{:S(2)}) collective-permute-start(bf16[64,2048]{1,0:T(8,128)(2,1)S(1)} %collective-permute-done.34.refs_3_), channel_id=1, source_target_pairs={{0,2},{1,3},{2,0},{3,1},{4,6},{5,7},{6,4},{7,5},{8,9},{9,8},{10,11... | collective-permute-start | bytes 786440 | tf_op jit(solution)/shard_map/cond/branch_1_fun/ppermute | solution.py:38
  39.0 4.9 %collective-permute-start.40 = (bf16[64,2048]{1,0:T(8,128)(2,1)S(1)}, bf16[64,2048]{1,0:T(8,128)(2,1)S(1)}, u32[]{:S(2)}, u32[]{:S(2)}) collective-permute-start(bf16[64,2048]{1,0:T(8,128)(2,1)S(1)} %collective-permute-done.32.refs_1_), channel_id=1, source_target_pairs={{0,8},{8,0},{1,9},{9,1},{2,10},{10,2},{3,11},{11,3},{4,12},{12,4},... | collective-permute-start | bytes 786440 | tf_op jit(solution)/shard_map/cond/branch_1_fun/ppermute | solution.py:42
  39.1 9.9 %collective-permute-start.44 = (bf16[64,2048]{1,0:T(8,128)(2,1)S(1)}, bf16[64,2048]{1,0:T(8,128)(2,1)S(1)}, u32[]{:S(2)}, u32[]{:S(2)}) collective-permute-start(bf16[64,2048]{1,0:T(8,128)(2,1)S(1)} %collective-permute-done.36.refs_5_), channel_id=1, source_target_pairs={{0,8},{8,0},{1,9},{9,1},{2,10},{10,2},{3,11},{11,3},{4,12},{12,4},... | collective-permute-start | bytes 786440 | tf_op jit(solution)/shard_map/cond/branch_1_fun/ppermute | solution.py:42
  39.7 9.3 %collective-permute-start.45 = (bf16[64,2048]{1,0:T(8,128)(2,1)S(1)}, bf16[64,2048]{1,0:T(8,128)(2,1)S(1)}, u32[]{:S(2)}, u32[]{:S(2)}) collective-permute-start(bf16[64,2048]{1,0:T(8,128)(2,1)S(1)} %collective-permute-done.37.refs_6_), channel_id=1, source_target_pairs={{0,8},{8,0},{1,9},{9,1},{2,10},{10,2},{3,11},{11,3},{4,12},{12,4},... | collective-permute-start | bytes 786440 | tf_op jit(solution)/shard_map/cond/branch_1_fun/ppermute | solution.py:42
  39.8 9.2 %collective-permute-start.42 = (bf16[64,2048]{1,0:T(8,128)(2,1)S(1)}, bf16[64,2048]{1,0:T(8,128)(2,1)S(1)}, u32[]{:S(2)}, u32[]{:S(2)}) collective-permute-start(bf16[64,2048]{1,0:T(8,128)(2,1)S(1)} %collective-permute-done.34.refs_3_), channel_id=1, source_target_pairs={{0,8},{8,0},{1,9},{9,1},{2,10},{10,2},{3,11},{11,3},{4,12},{12,4},... | collective-permute-start | bytes 786440 | tf_op jit(solution)/shard_map/cond/branch_1_fun/ppermute | solution.py:42
  43.2 5.8 %collective-permute-start.46 = (bf16[64,2048]{1,0:T(8,128)(2,1)S(1)}, bf16[64,2048]{1,0:T(8,128)(2,1)S(1)}, u32[]{:S(2)}, u32[]{:S(2)}) collective-permute-start(bf16[64,2048]{1,0:T(8,128)(2,1)S(1)} %collective-permute-done.38.refs_7_), channel_id=1, source_target_pairs={{0,8},{8,0},{1,9},{9,1},{2,10},{10,2},{3,11},{11,3},{4,12},{12,4},... | collective-permute-start | bytes 786440 | tf_op jit(solution)/shard_map/cond/branch_1_fun/ppermute | solution.py:42
  43.9 9.5 %collective-permute-start.48 = (bf16[128,1024]{1,0:T(8,128)(2,1)S(1)}, bf16[128,1024]{1,0:T(8,128)(2,1)S(1)}, u32[]{:S(2)}, u32[]{:S(2)}) collective-permute-start(bf16[128,1024]{1,0:T(8,128)(2,1)S(1)} %bitcast.35), channel_id=1, source_target_pairs={{1,0},{2,1},{3,2},{4,3},{5,4},{6,5},{7,6},{0,7},{9,8},{10,9},{11,1... | collective-permute-start | bytes 786440 | tf_op jit(solution)/shard_map/cond/branch_1_fun/ppermute | solution.py:46
  54.4 3.4 %collective-permute-start.51 = (bf16[256,1024]{1,0:T(8,128)(2,1)S(1)}, bf16[256,1024]{1,0:T(8,128)(2,1)S(1)}, u32[]{:S(2)}, u32[]{:S(2)}) collective-permute-start(bf16[256,1024]{1,0:T(8,128)(2,1)S(1)} %get-tuple-element.98), channel_id=1, source_target_pairs={{0,8},{8,0},{1,9},{9,1},{2,10},{10,2},{3,11},{11,3},{4,12},{12,4},... | collective-permute-start | bytes 1572872 | tf_op jit(solution)/shard_map/cond/branch_1_fun/ppermute | solution.py:42
  54.5 9.6 %collective-permute-start.47 = (bf16[128,512]{1,0:T(8,128)(2,1)S(1)}, bf16[128,512]{1,0:T(8,128)(2,1)S(1)}, u32[]{:S(2)}, u32[]{:S(2)}) collective-permute-start(bf16[128,512]{1,0:T(8,128)(2,1)S(1)} %slice.182), channel_id=1, source_target_pairs={{7,0},{0,1},{1,2},{2,3},{3,4},{4,5},{5,6},{6,7},{15,8},{8,9},{9,10... | collective-permute-start | bytes 393224 | tf_op jit(solution)/shard_map/cond/branch_1_fun/ppermute | solution.py:46
  57.2 10.3 %collective-permute-start.49 = (bf16[512,768]{1,0:T(8,128)(2,1)S(1)}, bf16[512,768]{1,0:T(8,128)(2,1)S(1)}, u32[]{:S(2)}, u32[]{:S(2)}) collective-permute-start(bf16[512,768]{1,0:T(8,128)(2,1)S(1)} %get-tuple-element.91), channel_id=1, source_target_pairs={{0,8},{8,0},{1,9},{9,1},{2,10},{10,2},{3,11},{11,3},{4,12},{12,4},... | collective-permute-start | bytes 2359304 | tf_op jit(solution)/shard_map/cond/branch_1_fun/ppermute | solution.py:42
  58.0 8.4 %collective-permute-start.59 = (bf16[128,1024]{1,0:T(8,128)(2,1)S(1)}, bf16[128,1024]{1,0:T(8,128)(2,1)S(1)}, u32[]{:S(2)}, u32[]{:S(2)}) collective-permute-start(bf16[128,1024]{1,0:T(8,128)(2,1)S(1)} %slice.293), channel_id=1, source_target_pairs={{0,2},{1,3},{2,0},{3,1},{4,6},{5,7},{6,4},{7,5},{8,9},{9,8},{10,11... | collective-permute-start | bytes 786440 | tf_op jit(solution)/shard_map/cond/branch_1_fun/ppermute | solution.py:38
  66.3 8.4 %collective-permute-start.55 = (bf16[512,768]{1,0:T(8,128)(2,1)S(1)}, bf16[512,768]{1,0:T(8,128)(2,1)S(1)}, u32[]{:S(2)}, u32[]{:S(2)}) collective-permute-start(bf16[512,768]{1,0:T(8,128)(2,1)S(1)} %get-tuple-element.104), channel_id=1, source_target_pairs={{0,8},{8,0},{1,9},{9,1},{2,10},{10,2},{3,11},{11,3},{4,12},{12,4},... | collective-permute-start | bytes 2359304 | tf_op jit(solution)/shard_map/cond/branch_1_fun/ppermute | solution.py:42
  66.5 6.4 %collective-permute-start.60 = (bf16[64,1024]{1,0:T(8,128)(2,1)S(1)}, bf16[64,1024]{1,0:T(8,128)(2,1)S(1)}, u32[]{:S(2)}, u32[]{:S(2)}) collective-permute-start(bf16[64,1024]{1,0:T(8,128)(2,1)S(1)} %slice.296), channel_id=1, source_target_pairs={{0,1},{1,0},{2,3},{3,2},{4,5},{5,4},{6,7},{7,6},{8,10},{9,11},{10,... | collective-permute-start | bytes 393224 | tf_op jit(solution)/shard_map/cond/branch_1_fun/ppermute | solution.py:38
  67.7 12.2 %collective-permute-start.50 = (bf16[256,768]{1,0:T(8,128)(2,1)S(1)}, bf16[256,768]{1,0:T(8,128)(2,1)S(1)}, u32[]{:S(2)}, u32[]{:S(2)}) collective-permute-start(bf16[256,768]{1,0:T(8,128)(2,1)S(1)} %slice.292), channel_id=1, source_target_pairs={{0,2},{1,3},{2,0},{3,1},{4,6},{5,7},{6,4},{7,5},{8,9},{9,8},{10,11... | collective-permute-start | bytes 1179656 | tf_op jit(solution)/shard_map/cond/branch_1_fun/ppermute | solution.py:38
  70.4 27.4 %collective-permute-start.52 = (bf16[128,1024]{1,0:T(8,128)(2,1)S(1)}, bf16[128,1024]{1,0:T(8,128)(2,1)S(1)}, u32[]{:S(2)}, u32[]{:S(2)}) collective-permute-start(bf16[128,1024]{1,0:T(8,128)(2,1)S(1)} %slice.230), channel_id=1, source_target_pairs={{7,0},{0,1},{1,2},{2,3},{3,4},{4,5},{5,6},{6,7},{15,8},{8,9},{9,10... | collective-permute-start | bytes 786440 | tf_op jit(solution)/shard_map/cond/branch_1_fun/ppermute | solution.py:46
  72.9 6.3 %collective-permute-start.61 = (bf16[32,1024]{1,0:T(8,128)(2,1)S(1)}, bf16[32,1024]{1,0:T(8,128)(2,1)S(1)}, u32[]{:S(2)}, u32[]{:S(2)}) collective-permute-start(bf16[32,1024]{1,0:T(8,128)(2,1)S(1)} %slice.299), channel_id=1, source_target_pairs={{0,4},{1,5},{2,6},{3,7},{4,0},{5,1},{6,2},{7,3},{8,12},{9,13},{10,... | collective-permute-start | bytes 196616 | tf_op jit(solution)/shard_map/cond/branch_1_fun/ppermute | solution.py:38
  74.9 10.9 %collective-permute-start.56 = (bf16[256,768]{1,0:T(8,128)(2,1)S(1)}, bf16[256,768]{1,0:T(8,128)(2,1)S(1)}, u32[]{:S(2)}, u32[]{:S(2)}) collective-permute-start(bf16[256,768]{1,0:T(8,128)(2,1)S(1)} %slice.291), channel_id=1, source_target_pairs={{0,2},{1,3},{2,0},{3,1},{4,6},{5,7},{6,4},{7,5},{8,9},{9,8},{10,11... | collective-permute-start | bytes 1179656 | tf_op jit(solution)/shard_map/cond/branch_1_fun/ppermute | solution.py:38
  80.0 10.6 %collective-permute-start.53 = (bf16[128,768]{1,0:T(8,128)(2,1)S(1)}, bf16[128,768]{1,0:T(8,128)(2,1)S(1)}, u32[]{:S(2)}, u32[]{:S(2)}) collective-permute-start(bf16[128,768]{1,0:T(8,128)(2,1)S(1)} %slice.295), channel_id=1, source_target_pairs={{0,1},{1,0},{2,3},{3,2},{4,5},{5,4},{6,7},{7,6},{8,10},{9,11},{10,... | collective-permute-start | bytes 589832 | tf_op jit(solution)/shard_map/cond/branch_1_fun/ppermute | solution.py:38
  85.9 8.4 %collective-permute-start.57 = (bf16[128,768]{1,0:T(8,128)(2,1)S(1)}, bf16[128,768]{1,0:T(8,128)(2,1)S(1)}, u32[]{:S(2)}, u32[]{:S(2)}) collective-permute-start(bf16[128,768]{1,0:T(8,128)(2,1)S(1)} %slice.294), channel_id=1, source_target_pairs={{0,1},{1,0},{2,3},{3,2},{4,5},{5,4},{6,7},{7,6},{8,10},{9,11},{10,... | collective-permute-start | bytes 589832 | tf_op jit(solution)/shard_map/cond/branch_1_fun/ppermute | solution.py:38
  90.7 9.9 %collective-permute-start.54 = (bf16[64,768]{1,0:T(8,128)(2,1)S(1)}, bf16[64,768]{1,0:T(8,128)(2,1)S(1)}, u32[]{:S(2)}, u32[]{:S(2)}) collective-permute-start(bf16[64,768]{1,0:T(8,128)(2,1)S(1)} %slice.298), channel_id=1, source_target_pairs={{0,4},{1,5},{2,6},{3,7},{4,0},{5,1},{6,2},{7,3},{8,12},{9,13},{10,... | collective-permute-start | bytes 294920 | tf_op jit(solution)/shard_map/cond/branch_1_fun/ppermute | solution.py:38
  94.4 6.3 %collective-permute-start.58 = (bf16[64,768]{1,0:T(8,128)(2,1)S(1)}, bf16[64,768]{1,0:T(8,128)(2,1)S(1)}, u32[]{:S(2)}, u32[]{:S(2)}) collective-permute-start(bf16[64,768]{1,0:T(8,128)(2,1)S(1)} %slice.297), channel_id=1, source_target_pairs={{0,4},{1,5},{2,6},{3,7},{4,0},{5,1},{6,2},{7,3},{8,12},{9,13},{10,... | collective-permute-start | bytes 294920 | tf_op jit(solution)/shard_map/cond/branch_1_fun/ppermute | solution.py:38
  (4 other events, 66.4 us)
where the time goes:
time: 103 us; the launch traced here: 101 us
  starting transfers between devices  41.8 us (41%)
  waiting for transfers between devices  32.4 us (31%)
  Pallas kernels  14.6 us (14%)
  other arithmetic  6.87 us (7%)
  local copies, waits for them, and re-layouts  3.81 us (4%)
  between operations  1.28 us (1%)
    ppermute x16, starting transfers between devices, exchange(): return lax.ppermute(block, ('fsdp', 'rows'), pairs)  30.2 us
    ppermute x16, waiting for transfers between devices, exchange(): return lax.ppermute(block, ('fsdp', 'rows'), pairs)  28.4 us
    ppermute x4, starting transfers between devices, shifted(): lax.ppermute(block, 'rows', [((i - distance) % rows, i) for i in range(ro...  9.75 us
    ppermute x4, waiting for transfers between devices, shifted(): lax.ppermute(block, 'rows', [((i - distance) % rows, i) for i in range(ro...  3.98 us
    pallas_call x1, Pallas kernels, branch(): call(functools.partial(forward_kernel, blocks=blocks), [((dim, 3 * hidden...  3.2 us
    pallas_call x1, Pallas kernels, branch(): call(backward_a_kernel, [((cells, hidden), BF16)] + half_outs, [VM] * 5,...  2.62 us
    pallas_call x1, Pallas kernels, branch(): call(backward_b_kernel, half_outs, [VM, VM, VM, VM], flops=4 * cells * di...  2.21 us
  transfers between devices with their start and end apart: 31, of which 10 were waited for; matrix products, arithmetic and copies ran while one was open for 9% of the time, Pallas kernels for 13%

commit v1 on v0

--- a/solution.py
+++ b/solution.py
@@ -238,10 +238,10 @@
     got_a = exchange(own, rows, a)
     got_b = exchange(own, rows, b)
     got_c = exchange(own, rows, c)
-    got_ab = exchange(after(got_a, got_b, halo), rows, b)
+    got_ab = exchange(after(got_a, got_b), rows, b)
     got_ac = exchange(after(got_a, got_c), rows, c)
     got_bc = exchange(after(got_b, got_c), rows, c)
-    got_abc = exchange(after(got_ab, got_ac), rows, c)
+    got_abc = exchange(after(got_ab, got_ac, halo), rows, c)
     held = (own, got_a, got_b, got_ab, got_c, got_ac, got_bc, got_abc)
     return held + tuple(swap_cores(x) for x in held)
 
@@ -297,11 +297,11 @@
     own_mask = cell_mask.astype(BF16).reshape(cells, 1)
     tile = 16
     mask_rows = jnp.pad(part(own_mask).T, ((0, tile - 1), (0, dim - half)))
-    halo = shifted(jnp.concatenate([part(own), mask_rows], axis=0), rows, distance)
+    halo = shifted(jnp.concatenate([part(own), mask_rows, part(own_cot)], axis=0), rows, distance)
     flat_out = jnp.concatenate([projection_out[:, : dim // 2], projection_out[:, dim // 2 :]], axis=0)
     both = jnp.concatenate([projection_in, flat_out], axis=1)
     in_parts = gather_pieces(both, rows, halo)
-    halo_cot = shifted(after(part(own_cot), in_parts[5], in_parts[6]), rows, distance)
+    halo_cot = halo[half + tile :]
     halo_mask = halo[half, :half][:, None]
 
     cell = jnp.arange(cells, dtype=jnp.int32)
@@ -337,7 +337,6 @@
         moved=10 << 20,
         name="fwd",
     )(table, table, normed_bf, bias, *in_parts)
-    back_ctx = shifted(part(ctx), rows, -distance)
     cot, keep_out, send_out = call(
         functools.partial(term_out_kernel, **shape_kw),
         [((cells, dim), BF16), ((hidden // 2, dim), F32), ((hidden // 2, dim), BF16)],
@@ -358,6 +357,7 @@
         name="bwd_a",
     )(cot, packed, attn, ordered, full_out)
     swapped_a = swap_cores(send_a)
+    back_ctx = shifted(after(part(ctx), gp_a), rows, -distance)
     gp_b, keep_b, send_b = call(
         backward_b_kernel,
         half_outs,
@@ -365,7 +365,7 @@
         flops=4 * cells * dim * 3 * hidden,
         moved=6 << 20,
         name="bwd_b",
-    )(packed, attn, after(gctx, swapped_out, back_ctx), ordered)
+    )(packed, attn, after(gctx, swapped_out), ordered)
     swapped_b = swap_cores(send_b)
     kept_out, last_out, _, _ = scatter_from(keep_out, swapped_out, rows)
     grad_out = kept_out + last_out.astype(F32)

time: 103 us -> 98.2 us (0.953); the launches traced: 101 us -> 98.4 us
  starting transfers between devices: 41.8 us -> 22.8 us
  waiting for transfers between devices: 32.4 us -> 48.4 us
    ppermute x16, waiting for transfers between devices: 28.4 us -> 48.3 us  [exchange(): return lax.ppermute(block, ('fsdp', 'rows'), pairs)]
    ppermute x16, starting transfers between devices: 30.2 us -> 13.8 us  [exchange(): return lax.ppermute(block, ('fsdp', 'rows'), pairs)]
    ppermute x4 -> x3, starting transfers between devices: 9.75 us -> 4.58 us  [shifted(): lax.ppermute(block, 'rows', [((i - distance) % rows, i) for i in range(ro...]
    ppermute x4 -> x3, waiting for transfers between devices: 3.98 us -> 0.01 us  [shifted(): lax.ppermute(block, 'rows', [((i - distance) % rows, i) for i in range(ro...]
    ppermute x11, starting transfers between devices: 1.85 us -> 4.5 us  [swap_cores(): return lax.ppermute(block, 'fsdp', [(0, 1), (1, 0)])]
  transfers between devices with their start and end apart: 31 -> 30, of which waited for: 10 -> 9; matrix products, arithmetic and copies ran while one was open for 9% -> 9% of each run, Pallas kernels for 13% -> 10%
where the time goes in v1:
time: 98.2 us; the launch traced here: 98.4 us
  waiting for transfers between devices  48.4 us (49%)
  starting transfers between devices  22.8 us (23%)
  Pallas kernels  14.5 us (15%)
  other arithmetic  7.01 us (7%)
  local copies, waits for them, and re-layouts  3.84 us (4%)
  between operations  1.28 us (1%)
    ppermute x16, waiting for transfers between devices, exchange(): return lax.ppermute(block, ('fsdp', 'rows'), pairs)  48.3 us
    ppermute x16, starting transfers between devices, exchange(): return lax.ppermute(block, ('fsdp', 'rows'), pairs)  13.8 us
    ppermute x3, starting transfers between devices, shifted(): lax.ppermute(block, 'rows', [((i - distance) % rows, i) for i in range(ro...  4.58 us
    ppermute x11, starting transfers between devices, swap_cores(): return lax.ppermute(block, 'fsdp', [(0, 1), (1, 0)])  4.5 us
    pallas_call x1, Pallas kernels, branch(): call(functools.partial(forward_kernel, blocks=blocks), [((dim, 3 * hidden...  3.2 us
    pallas_call x1, Pallas kernels, branch(): call(backward_a_kernel, [((cells, hidden), BF16)] + half_outs, [VM] * 5,...  2.62 us
    pallas_call x1, Pallas kernels, branch(): call(backward_b_kernel, half_outs, [VM, VM, VM, VM], flops=4 * cells * di...  2.21 us
    slice x5, local copies, waits for them, and re-layouts, branch(): part = lambda a: lax.slice_in_dim(a, low, low + half, axis=0)  1.97 us
  transfers between devices with their start and end apart: 30, of which 9 were waited for; matrix products, arithmetic and copies ran while one was open for 9% of the time, Pallas kernels for 10%

profile of v1, /device:TPU:0, one launch (start us, length us, event | category | flops | bytes accessed | tf_op | source)
XLA Modules:
  0.0 98.4 jit_solution(9447425094159822952)
XLA Ops:
  1.3 97.1 %conditional.1 = (bf16[1,16,16,1024]{3,2,1,0:T(8,128)(2,1)}, bf16[1,16,16,1024]{3,2,1,0:T(8,128)(2,1)}, f32[64,1536]{1,0:T(8,128)}, f32[32,1024]{1,0:T(8,128)}) conditional(s32[]{:T(128)} %bitcast.18, (bf16[1,16,16,1024]{3,2,1,0:T(8,128)(2,1)}, s32[8]{0:T(128)}, s32[8]{0:T(128)}, s32[1,16,16]{2,1,0:T(8,128)}, bf16[1,16,16,1024]{3,2,1,0:T(8,128)(2,1)}, ...), branch_computations={%region_0.1_spmd, %region_1.2_spmd} | conditional | flops 6992472064 | bytes 108641328 | solution.py:406
  2.1 0.9 maximum_maximum_fusion.refs_0_
  3.1 4.1 %collective-permute-start.1 = (bf16[64,2048]{1,0:T(8,128)(2,1)S(1)}, bf16[64,2048]{1,0:T(8,128)(2,1)S(1)}, u32[]{:S(2)}, u32[]{:S(2)}) collective-permute-start(bf16[64,2048]{1,0:T(8,128)(2,1)S(1)} %maximum_maximum_fusion.refs_0_), channel_id=1, source_target_pairs={{0,4},{1,5},{2,6},{3,7},{4,0},{5,1},{6,2},{7,3},{8,12},{9,13},{10,... | collective-permute-start | bytes 786440 | tf_op jit(solution)/shard_map/cond/branch_0_fun/ppermute | solution.py:38
  7.2 1.5 %collective-permute-start.2 = (bf16[64,2048]{1,0:T(8,128)(2,1)S(1)}, bf16[64,2048]{1,0:T(8,128)(2,1)S(1)}, u32[]{:S(2)}, u32[]{:S(2)}) collective-permute-start(bf16[64,2048]{1,0:T(8,128)(2,1)S(1)} %maximum_maximum_fusion.refs_0_), channel_id=1, source_target_pairs={{0,1},{1,0},{2,3},{3,2},{4,5},{5,4},{6,7},{7,6},{8,10},{9,11},{10,... | collective-permute-start | bytes 786440 | tf_op jit(solution)/shard_map/cond/branch_0_fun/ppermute | solution.py:38
  8.7 1.6 %collective-permute-start.4 = (bf16[64,2048]{1,0:T(8,128)(2,1)S(1)}, bf16[64,2048]{1,0:T(8,128)(2,1)S(1)}, u32[]{:S(2)}, u32[]{:S(2)}) collective-permute-start(bf16[64,2048]{1,0:T(8,128)(2,1)S(1)} %maximum_maximum_fusion.refs_0_), channel_id=1, source_target_pairs={{0,2},{1,3},{2,0},{3,1},{4,6},{5,7},{6,4},{7,5},{8,9},{9,8},{10,11... | collective-permute-start | bytes 786440 | tf_op jit(solution)/shard_map/cond/branch_0_fun/ppermute | solution.py:38
  10.3 1.0 slice.148
  11.3 1.0 slice.151
  12.3 0.9 fusion.3
  14.3 4.9 %collective-permute-done.1.refs_1_ = bf16[64,2048]{1,0:T(8,128)(2,1)S(1)} collective-permute-done((bf16[64,2048]{1,0:T(8,128)(2,1)S(1)}, bf16[64,2048]{1,0:T(8,128)(2,1)S(1)}, u32[]{:S(2)}, u32[]{:S(2)}) %collective-permute-start.1) | collective-permute-done | bytes 262176 | tf_op jit(solution)/shard_map/cond/branch_0_fun/ppermute | solution.py:38
  19.2 1.7 %collective-permute-start.3 = (bf16[64,2048]{1,0:T(8,128)(2,1)S(1)}, bf16[64,2048]{1,0:T(8,128)(2,1)S(1)}, u32[]{:S(2)}, u32[]{:S(2)}) collective-permute-start(bf16[64,2048]{1,0:T(8,128)(2,1)S(1)} %collective-permute-done.1.refs_1_), channel_id=1, source_target_pairs={{0,1},{1,0},{2,3},{3,2},{4,5},{5,4},{6,7},{7,6},{8,10},{9,11},{10,... | collective-permute-start | bytes 786440 | tf_op jit(solution)/shard_map/cond/branch_0_fun/ppermute | solution.py:38
  21.5 1.3 %fusion.9 = s32[256]{0:T(256)S(1)} fusion(pred[]{:T(512)S(6)} %eq.37, s32[]{:T(128)} %bitcast.4, s32[]{:T(128)} %bitcast.3), kind=kLoop, calls=%fused_computation.40 | loop fusion | flops 4608 | bytes 1033 | tf_op jit(solution)/shard_map/cond/branch_0_fun/add | solution.py:313
  22.8 1.5 %collective-permute-start.6 = (bf16[64,2048]{1,0:T(8,128)(2,1)S(1)}, bf16[64,2048]{1,0:T(8,128)(2,1)S(1)}, u32[]{:S(2)}, u32[]{:S(2)}) collective-permute-start(bf16[64,2048]{1,0:T(8,128)(2,1)S(1)} %collective-permute-done.2.refs_2_), channel_id=1, source_target_pairs={{0,2},{1,3},{2,0},{3,1},{4,6},{5,7},{6,4},{7,5},{8,9},{9,8},{10,11... | collective-permute-start | bytes 786440 | tf_op jit(solution)/shard_map/cond/branch_0_fun/ppermute | solution.py:38
  24.3 14.5 %collective-permute-done.3.refs_3_ = bf16[64,2048]{1,0:T(8,128)(2,1)S(1)} collective-permute-done((bf16[64,2048]{1,0:T(8,128)(2,1)S(1)}, bf16[64,2048]{1,0:T(8,128)(2,1)S(1)}, u32[]{:S(2)}, u32[]{:S(2)}) %collective-permute-start.3) | collective-permute-done | bytes 262176 | tf_op jit(solution)/shard_map/cond/branch_0_fun/ppermute | solution.py:38
  40.3 1.0 %collective-permute-start.11 = (bf16[64,2048]{1,0:T(8,128)(2,1)S(1)}, bf16[64,2048]{1,0:T(8,128)(2,1)S(1)}, u32[]{:S(2)}, u32[]{:S(2)}) collective-permute-start(bf16[64,2048]{1,0:T(8,128)(2,1)S(1)} %collective-permute-done.3.refs_3_), channel_id=1, source_target_pairs={{0,8},{8,0},{1,9},{9,1},{2,10},{10,2},{3,11},{11,3},{4,12},{12,4},... | collective-permute-start | bytes 786440 | tf_op jit(solution)/shard_map/cond/branch_0_fun/ppermute | solution.py:42
  41.8 3.9 %collective-permute-done.7.refs_7_ = bf16[64,2048]{1,0:T(8,128)(2,1)S(1)} collective-permute-done((bf16[64,2048]{1,0:T(8,128)(2,1)S(1)}, bf16[64,2048]{1,0:T(8,128)(2,1)S(1)}, u32[]{:S(2)}, u32[]{:S(2)}) %collective-permute-start.7) | collective-permute-done | bytes 262176 | tf_op jit(solution)/shard_map/cond/branch_0_fun/ppermute | solution.py:38
  46.4 1.7 %norm.2 = (bf16[256,1024]{1,0:T(8,128)(2,1)S(1)}, bf16[256,1024]{1,0:T(8,128)(2,1)S(1)}, bf16[1024,256]{1,0:T(8,128)(2,1)S(1)}, f32[256,1]{1,0:T(8,128)S(1)}, f32[256,1]{1,0:T(8,128)S(1)}) custom-call(s32[2]{0:T(128)S(1)} %copy-done.4, s32[16]{0:T(128)S(1)} %pad_add_fusion.table.place_at.order, bf16[256,1024]{1,0:T(8,128)(2,1)} %bitcast.22, ...), custom_call_target="tpu_custom_call" | custom-call | flops 5242880 | bytes 2621440 | tf_op jit(solution)/shard_map/cond/branch_0_fun/norm/pallas_call | solution.py:322
  48.3 3.2 %fwd.2 = (bf16[1024,1536]{1,0:T(8,128)(2,1)S(1)}, bf16[512,1024]{1,0:T(8,128)(2,1)S(1)}, bf16[256,1536]{1,0:T(8,128)(2,1)S(1)}, f32[8,256,256]{2,1,0:T(8,128)S(1...) custom-call(s32[16]{0:T(128)S(1)} %pad_add_fusion.table.place_at.order, ...), custom_call_target="tpu_custom_call" | custom-call | flops 2415919104 | bytes 10485760 | tf_op jit(solution)/shard_map/cond/branch_0_fun/fwd/pallas_call | solution.py:331
  51.5 1.0 %term_out.2 = (bf16[256,1024]{1,0:T(8,128)(2,1)S(1)}, f32[256,1024]{1,0:T(8,128)S(1)}, bf16[256,1024]{1,0:T(8,128)(2,1)S(1)}) custom-call(s32[2]{0:T(128)S(1)} %copy-done.4, bf16[512,256]{1,0:T(8,128)(2,1)S(1)} %get-tuple-element.46.ctx_ordered, bf16[256,1024]{1,0:T(8,128)(2,1)S(1)} %bitcast.26, bf16[128,1024]{1,0:T(8,128)(2,1)S(1)} %slice.214.halo), custom_call_target="tpu_custom_call" | custom-call | flops 268435456 | bytes 4194304 | tf_op jit(solution)/shard_map/cond/branch_0_fun/term_out/pallas_call | solution.py:340
  53.1 2.6 %bwd_a.2 = (bf16[256,512]{1,0:T(8,128)(2,1)S(1)}, bf16[256,768]{1,0:T(8,128)(2,1)S(1)}, f32[512,768]{1,0:T(8,128)S(1)}, bf16[512,768]{1,0:T(8,128)(2,1)S(1)}) custom-call(bf16[256,1024]{1,0:T(8,128)(2,1)S(1)} %get-tuple-element.47.cot, bf16[256,1536]{1,0:T(8,128)(2,1)S(1)} %get-tuple-element.48.packed, f32[8,256,256]{2,1,0:T(8,128)S(1)} %get-tuple-element.49.attn, ...), custom_call_target="tpu_custom_call" | custom-call | flops 1610612736 | bytes 6291456 | tf_op jit(solution)/shard_map/cond/branch_0_fun/bwd_a/pallas_call | solution.py:351
  57.4 0.8 collective-permute-start.16
  58.2 2.2 %bwd_b.2 = (bf16[256,768]{1,0:T(8,128)(2,1)S(1)}, f32[512,768]{1,0:T(8,128)S(1)}, bf16[512,768]{1,0:T(8,128)(2,1)S(1)}) custom-call(bf16[256,1536]{1,0:T(8,128)(2,1)S(1)} %get-tuple-element.48.packed, f32[8,256,256]{2,1,0:T(8,128)S(1)} %get-tuple-element.49.attn, bf16[256,512]{1,0:T(8,128)(2,1)S(1)} %get-tuple-element.62.gctx, ...), custom_call_target="tpu_custom_call" | custom-call | flops 1610612736 | bytes 6291456 | tf_op jit(solution)/shard_map/cond/branch_0_fun/bwd_b/pallas_call | solution.py:361
  60.4 1.7 %collective-permute-start.23 = (bf16[512,768]{1,0:T(8,128)(2,1)S(1)}, bf16[512,768]{1,0:T(8,128)(2,1)S(1)}, u32[]{:S(2)}, u32[]{:S(2)}) collective-permute-start(bf16[512,768]{1,0:T(8,128)(2,1)S(1)} %get-tuple-element.67), channel_id=1, source_target_pairs={{0,8},{8,0},{1,9},{9,1},{2,10},{10,2},{3,11},{11,3},{4,12},{12,4},... | collective-permute-start | bytes 2359304 | tf_op jit(solution)/shard_map/cond/branch_0_fun/ppermute | solution.py:42
  62.2 1.6 %collective-permute-done.27 = bf16[128,1024]{1,0:T(8,128)(2,1)S(1)} collective-permute-done((bf16[128,1024]{1,0:T(8,128)(2,1)S(1)}, bf16[128,1024]{1,0:T(8,128)(2,1)S(1)}, u32[]{:S(2)}, u32[]{:S(2)}) %collective-permute-start.27) | collective-permute-done | bytes 262176 | tf_op jit(solution)/shard_map/cond/branch_0_fun/ppermute | solution.py:38
  64.2 1.3 %grad.2 = bf16[256,1024]{1,0:T(8,128)(2,1)S(1)} custom-call(bf16[256,1024]{1,0:T(8,128)(2,1)S(1)} %get-tuple-element.57.xw, f32[256,1]{1,0:T(8,128)S(1)} %get-tuple-element.58.mean, f32[256,1]{1,0:T(8,128)S(1)} %get-tuple-element.59.inv, bf16[256,768]{1,0:T(8,128)(2,1)S(1)} %get-tuple-element.52.gp_a, bf16[256,768]{1,0:T(8,128)(2,1)S(1)} %get-tuple-element.64.gp_b, ...), custom_call_target="tpu_custom_call" | custom-call | flops 805306368 | bytes 6291456 | tf_op jit(solution)/shard_map/cond/branch_0_fun/grad/pallas_call | solution.py:381
  65.5 3.3 %collective-permute-start.20 = (bf16[128,1024]{1,0:T(8,128)(2,1)S(1)}, bf16[128,1024]{1,0:T(8,128)(2,1)S(1)}, u32[]{:S(2)}, u32[]{:S(2)}) collective-permute-start(bf16[128,1024]{1,0:T(8,128)(2,1)S(1)} %slice.216), channel_id=1, source_target_pairs={{1,0},{2,1},{3,2},{4,3},{5,4},{6,5},{7,6},{0,7},{9,8},{10,9},{11,1... | collective-permute-start | bytes 786440 | tf_op jit(solution)/shard_map/cond/branch_0_fun/ppermute | solution.py:46
  68.8 1.5 %collective-permute-done.28 = bf16[64,1024]{1,0:T(8,128)(2,1)S(1)} collective-permute-done((bf16[64,1024]{1,0:T(8,128)(2,1)S(1)}, bf16[64,1024]{1,0:T(8,128)(2,1)S(1)}, u32[]{:S(2)}, u32[]{:S(2)}) %collective-permute-start.28) | collective-permute-done | bytes 131104 | tf_op jit(solution)/shard_map/cond/branch_0_fun/ppermute | solution.py:38
  71.3 6.0 %collective-permute-done.29 = bf16[32,1024]{1,0:T(8,128)(2,1)S(1)} collective-permute-done((bf16[32,1024]{1,0:T(8,128)(2,1)S(1)}, bf16[32,1024]{1,0:T(8,128)(2,1)S(1)}, u32[]{:S(2)}, u32[]{:S(2)}) %collective-permute-start.29) | collective-permute-done | bytes 65568 | tf_op jit(solution)/shard_map/cond/branch_0_fun/ppermute | solution.py:38
  78.2 7.9 %collective-permute-done.24 = bf16[256,768]{1,0:T(8,128)(2,1)S(1)} collective-permute-done((bf16[256,768]{1,0:T(8,128)(2,1)S(1)}, bf16[256,768]{1,0:T(8,128)(2,1)S(1)}, u32[]{:S(2)}, u32[]{:S(2)}) %collective-permute-start.24) | collective-permute-done | bytes 393248 | tf_op jit(solution)/shard_map/cond/branch_0_fun/ppermute | solution.py:38
  86.7 5.2 %collective-permute-done.25 = bf16[128,768]{1,0:T(8,128)(2,1)S(1)} collective-permute-done((bf16[128,768]{1,0:T(8,128)(2,1)S(1)}, bf16[128,768]{1,0:T(8,128)(2,1)S(1)}, u32[]{:S(2)}, u32[]{:S(2)}) %collective-permute-start.25) | collective-permute-done | bytes 196640 | tf_op jit(solution)/shard_map/cond/branch_0_fun/ppermute | solution.py:38
  92.1 1.0 pad_select_fusion
  93.1 1.8 %output.2 = bf16[256,1024]{1,0:T(8,128)(2,1)} custom-call(s32[2]{0:T(128)S(1)} %copy-done.4, bf16[256,1024]{1,0:T(8,128)(2,1)S(1)} %bitcast.23, bf16[256,512]{1,0:T(8,128)(2,1)S(1)} %get-tuple-element.45.ctx, bf16[128,512]{1,0:T(8,128)(2,1)S(1)} %collective-permute-done.16.back, bf16[512,1024]{1,0:T(8,128)(2,1)S(1)} %get-tuple-element.51.full), custom_call_target="tpu_custom_call" | custom-call | flops 268435456 | bytes 3145728 | tf_op jit(solution)/shard_map/cond/branch_0_fun/output/pallas_call | solution.py:391
  94.9 2.7 %collective-permute-done.26.last_b = bf16[64,768]{1,0:T(8,128)(2,1)S(1)} collective-permute-done((bf16[64,768]{1,0:T(8,128)(2,1)S(1)}, bf16[64,768]{1,0:T(8,128)(2,1)S(1)}, u32[]{:S(2)}, u32[]{:S(2)}) %collective-permute-start.26) | collective-permute-done | bytes 98336 | tf_op jit(solution)/shard_map/cond/branch_0_fun/ppermute | solution.py:38
  (92 shorter events, 11.4 us)
Async XLA Ops:
  1.3 21.5 %copy-start.8 = (s32[8]{0:T(128)S(1)}, s32[8]{0:T(128)}, u32[]{:S(2)}) copy-start(s32[8]{0:T(128)} %get-tuple-element.34) | copy-start | bytes 100 | tf_op jit(solution)/shard_map/cond
  1.3 21.5 %copy-start.10 = (s32[8]{0:T(128)S(1)}, s32[8]{0:T(128)}, u32[]{:S(2)}) copy-start(s32[8]{0:T(128)} %get-tuple-element.35) | copy-start | bytes 100 | tf_op jit(solution)/shard_map/cond
  3.1 16.1 %collective-permute-start.1 = (bf16[64,2048]{1,0:T(8,128)(2,1)S(1)}, bf16[64,2048]{1,0:T(8,128)(2,1)S(1)}, u32[]{:S(2)}, u32[]{:S(2)}) collective-permute-start(bf16[64,2048]{1,0:T(8,128)(2,1)S(1)} %maximum_maximum_fusion.refs_0_), channel_id=1, source_target_pairs={{0,4},{1,5},{2,6},{3,7},{4,0},{5,1},{6,2},{7,3},{8,12},{9,13},{10,... | collective-permute-start | bytes 786440 | tf_op jit(solution)/shard_map/cond/branch_0_fun/ppermute | solution.py:38
  7.2 12.0 %collective-permute-start.2 = (bf16[64,2048]{1,0:T(8,128)(2,1)S(1)}, bf16[64,2048]{1,0:T(8,128)(2,1)S(1)}, u32[]{:S(2)}, u32[]{:S(2)}) collective-permute-start(bf16[64,2048]{1,0:T(8,128)(2,1)S(1)} %maximum_maximum_fusion.refs_0_), channel_id=1, source_target_pairs={{0,1},{1,0},{2,3},{3,2},{4,5},{5,4},{6,7},{7,6},{8,10},{9,11},{10,... | collective-permute-start | bytes 786440 | tf_op jit(solution)/shard_map/cond/branch_0_fun/ppermute | solution.py:38
  8.7 12.2 %collective-permute-start.4 = (bf16[64,2048]{1,0:T(8,128)(2,1)S(1)}, bf16[64,2048]{1,0:T(8,128)(2,1)S(1)}, u32[]{:S(2)}, u32[]{:S(2)}) collective-permute-start(bf16[64,2048]{1,0:T(8,128)(2,1)S(1)} %maximum_maximum_fusion.refs_0_), channel_id=1, source_target_pairs={{0,2},{1,3},{2,0},{3,1},{4,6},{5,7},{6,4},{7,5},{8,9},{9,8},{10,11... | collective-permute-start | bytes 786440 | tf_op jit(solution)/shard_map/cond/branch_0_fun/ppermute | solution.py:38
  13.2 26.1 %collective-permute-start = (bf16[272,1024]{1,0:T(8,128)(2,1)}, bf16[272,1024]{1,0:T(8,128)(2,1)S(1)}, u32[]{:S(2)}, u32[]{:S(2)}) collective-permute-start(bf16[272,1024]{1,0:T(8,128)(2,1)} %fusion.3), channel_id=1, source_target_pairs={{7,0},{0,1},{1,2},{2,3},{3,4},{4,5},{5,6},{6,7},{15,8},{8,9},{9,10... | collective-permute-start | bytes 1671176 | tf_op jit(solution)/shard_map/cond/branch_0_fun/ppermute | solution.py:46
  13.7 26.5 %collective-permute-start.8 = (bf16[64,2048]{1,0:T(8,128)(2,1)S(1)}, bf16[64,2048]{1,0:T(8,128)(2,1)S(1)}, u32[]{:S(2)}, u32[]{:S(2)}) collective-permute-start(bf16[64,2048]{1,0:T(8,128)(2,1)S(1)} %maximum_maximum_fusion.refs_0_), channel_id=1, source_target_pairs={{0,8},{8,0},{1,9},{9,1},{2,10},{10,2},{3,11},{11,3},{4,12},{12,4},... | collective-permute-start | bytes 786440 | tf_op jit(solution)/shard_map/cond/branch_0_fun/ppermute | solution.py:42
  19.2 19.6 %collective-permute-start.3 = (bf16[64,2048]{1,0:T(8,128)(2,1)S(1)}, bf16[64,2048]{1,0:T(8,128)(2,1)S(1)}, u32[]{:S(2)}, u32[]{:S(2)}) collective-permute-start(bf16[64,2048]{1,0:T(8,128)(2,1)S(1)} %collective-permute-done.1.refs_1_), channel_id=1, source_target_pairs={{0,1},{1,0},{2,3},{3,2},{4,5},{5,4},{6,7},{7,6},{8,10},{9,11},{10,... | collective-permute-start | bytes 786440 | tf_op jit(solution)/shard_map/cond/branch_0_fun/ppermute | solution.py:38
  20.9 18.0 %collective-permute-start.5 = (bf16[64,2048]{1,0:T(8,128)(2,1)S(1)}, bf16[64,2048]{1,0:T(8,128)(2,1)S(1)}, u32[]{:S(2)}, u32[]{:S(2)}) collective-permute-start(bf16[64,2048]{1,0:T(8,128)(2,1)S(1)} %collective-permute-done.1.refs_1_), channel_id=1, source_target_pairs={{0,2},{1,3},{2,0},{3,1},{4,6},{5,7},{6,4},{7,5},{8,9},{9,8},{10,11... | collective-permute-start | bytes 786440 | tf_op jit(solution)/shard_map/cond/branch_0_fun/ppermute | solution.py:38
  22.8 17.5 %collective-permute-start.6 = (bf16[64,2048]{1,0:T(8,128)(2,1)S(1)}, bf16[64,2048]{1,0:T(8,128)(2,1)S(1)}, u32[]{:S(2)}, u32[]{:S(2)}) collective-permute-start(bf16[64,2048]{1,0:T(8,128)(2,1)S(1)} %collective-permute-done.2.refs_2_), channel_id=1, source_target_pairs={{0,2},{1,3},{2,0},{3,1},{4,6},{5,7},{6,4},{7,5},{8,9},{9,8},{10,11... | collective-permute-start | bytes 786440 | tf_op jit(solution)/shard_map/cond/branch_0_fun/ppermute | solution.py:38
  38.8 2.5 %collective-permute-start.10 = (bf16[64,2048]{1,0:T(8,128)(2,1)S(1)}, bf16[64,2048]{1,0:T(8,128)(2,1)S(1)}, u32[]{:S(2)}, u32[]{:S(2)}) collective-permute-start(bf16[64,2048]{1,0:T(8,128)(2,1)S(1)} %collective-permute-done.2.refs_2_), channel_id=1, source_target_pairs={{0,8},{8,0},{1,9},{9,1},{2,10},{10,2},{3,11},{11,3},{4,12},{12,4},... | collective-permute-start | bytes 786440 | tf_op jit(solution)/shard_map/cond/branch_0_fun/ppermute | solution.py:42
  38.8 2.5 %collective-permute-start.12 = (bf16[64,2048]{1,0:T(8,128)(2,1)S(1)}, bf16[64,2048]{1,0:T(8,128)(2,1)S(1)}, u32[]{:S(2)}, u32[]{:S(2)}) collective-permute-start(bf16[64,2048]{1,0:T(8,128)(2,1)S(1)} %collective-permute-done.4.refs_4_), channel_id=1, source_target_pairs={{0,8},{8,0},{1,9},{9,1},{2,10},{10,2},{3,11},{11,3},{4,12},{12,4},... | collective-permute-start | bytes 786440 | tf_op jit(solution)/shard_map/cond/branch_0_fun/ppermute | solution.py:42
  39.3 6.4 %collective-permute-start.7 = (bf16[64,2048]{1,0:T(8,128)(2,1)S(1)}, bf16[64,2048]{1,0:T(8,128)(2,1)S(1)}, u32[]{:S(2)}, u32[]{:S(2)}) collective-permute-start(bf16[64,2048]{1,0:T(8,128)(2,1)S(1)} %collective-permute-done.3.refs_3_), channel_id=1, source_target_pairs={{0,2},{1,3},{2,0},{3,1},{4,6},{5,7},{6,4},{7,5},{8,9},{9,8},{10,11... | collective-permute-start | bytes 786440 | tf_op jit(solution)/shard_map/cond/branch_0_fun/ppermute | solution.py:38
  40.2 8.0 %collective-permute-start.9 = (bf16[64,2048]{1,0:T(8,128)(2,1)S(1)}, bf16[64,2048]{1,0:T(8,128)(2,1)S(1)}, u32[]{:S(2)}, u32[]{:S(2)}) collective-permute-start(bf16[64,2048]{1,0:T(8,128)(2,1)S(1)} %collective-permute-done.1.refs_1_), channel_id=1, source_target_pairs={{0,8},{8,0},{1,9},{9,1},{2,10},{10,2},{3,11},{11,3},{4,12},{12,4},... | collective-permute-start | bytes 786440 | tf_op jit(solution)/shard_map/cond/branch_0_fun/ppermute | solution.py:42
  40.3 7.9 %collective-permute-start.11 = (bf16[64,2048]{1,0:T(8,128)(2,1)S(1)}, bf16[64,2048]{1,0:T(8,128)(2,1)S(1)}, u32[]{:S(2)}, u32[]{:S(2)}) collective-permute-start(bf16[64,2048]{1,0:T(8,128)(2,1)S(1)} %collective-permute-done.3.refs_3_), channel_id=1, source_target_pairs={{0,8},{8,0},{1,9},{9,1},{2,10},{10,2},{3,11},{11,3},{4,12},{12,4},... | collective-permute-start | bytes 786440 | tf_op jit(solution)/shard_map/cond/branch_0_fun/ppermute | solution.py:42
  41.3 6.9 %collective-permute-start.13 = (bf16[64,2048]{1,0:T(8,128)(2,1)S(1)}, bf16[64,2048]{1,0:T(8,128)(2,1)S(1)}, u32[]{:S(2)}, u32[]{:S(2)}) collective-permute-start(bf16[64,2048]{1,0:T(8,128)(2,1)S(1)} %collective-permute-done.5.refs_5_), channel_id=1, source_target_pairs={{0,8},{8,0},{1,9},{9,1},{2,10},{10,2},{3,11},{11,3},{4,12},{12,4},... | collective-permute-start | bytes 786440 | tf_op jit(solution)/shard_map/cond/branch_0_fun/ppermute | solution.py:42
  41.3 6.9 %collective-permute-start.14 = (bf16[64,2048]{1,0:T(8,128)(2,1)S(1)}, bf16[64,2048]{1,0:T(8,128)(2,1)S(1)}, u32[]{:S(2)}, u32[]{:S(2)}) collective-permute-start(bf16[64,2048]{1,0:T(8,128)(2,1)S(1)} %collective-permute-done.6.refs_6_), channel_id=1, source_target_pairs={{0,8},{8,0},{1,9},{9,1},{2,10},{10,2},{3,11},{11,3},{4,12},{12,4},... | collective-permute-start | bytes 786440 | tf_op jit(solution)/shard_map/cond/branch_0_fun/ppermute | solution.py:42
  45.7 2.5 %collective-permute-start.15 = (bf16[64,2048]{1,0:T(8,128)(2,1)S(1)}, bf16[64,2048]{1,0:T(8,128)(2,1)S(1)}, u32[]{:S(2)}, u32[]{:S(2)}) collective-permute-start(bf16[64,2048]{1,0:T(8,128)(2,1)S(1)} %collective-permute-done.7.refs_7_), channel_id=1, source_target_pairs={{0,8},{8,0},{1,9},{9,1},{2,10},{10,2},{3,11},{11,3},{4,12},{12,4},... | collective-permute-start | bytes 786440 | tf_op jit(solution)/shard_map/cond/branch_0_fun/ppermute | solution.py:42
  52.5 3.3 %collective-permute-start.19 = (bf16[256,1024]{1,0:T(8,128)(2,1)S(1)}, bf16[256,1024]{1,0:T(8,128)(2,1)S(1)}, u32[]{:S(2)}, u32[]{:S(2)}) collective-permute-start(bf16[256,1024]{1,0:T(8,128)(2,1)S(1)} %get-tuple-element.61), channel_id=1, source_target_pairs={{0,8},{8,0},{1,9},{9,1},{2,10},{10,2},{3,11},{11,3},{4,12},{12,4},... | collective-permute-start | bytes 1572872 | tf_op jit(solution)/shard_map/cond/branch_0_fun/ppermute | solution.py:42
  55.7 8.2 %collective-permute-start.17 = (bf16[512,768]{1,0:T(8,128)(2,1)S(1)}, bf16[512,768]{1,0:T(8,128)(2,1)S(1)}, u32[]{:S(2)}, u32[]{:S(2)}) collective-permute-start(bf16[512,768]{1,0:T(8,128)(2,1)S(1)} %get-tuple-element.55), channel_id=1, source_target_pairs={{0,8},{8,0},{1,9},{9,1},{2,10},{10,2},{3,11},{11,3},{4,12},{12,4},... | collective-permute-start | bytes 2359304 | tf_op jit(solution)/shard_map/cond/branch_0_fun/ppermute | solution.py:42
  56.0 7.8 %collective-permute-start.27 = (bf16[128,1024]{1,0:T(8,128)(2,1)S(1)}, bf16[128,1024]{1,0:T(8,128)(2,1)S(1)}, u32[]{:S(2)}, u32[]{:S(2)}) collective-permute-start(bf16[128,1024]{1,0:T(8,128)(2,1)S(1)} %slice.292), channel_id=1, source_target_pairs={{0,2},{1,3},{2,0},{3,1},{4,6},{5,7},{6,4},{7,5},{8,9},{9,8},{10,11... | collective-permute-start | bytes 786440 | tf_op jit(solution)/shard_map/cond/branch_0_fun/ppermute | solution.py:38
  57.4 35.7 %collective-permute-start.16 = (bf16[128,512]{1,0:T(8,128)(2,1)S(1)}, bf16[128,512]{1,0:T(8,128)(2,1)S(1)}, u32[]{:S(2)}, u32[]{:S(2)}) collective-permute-start(bf16[128,512]{1,0:T(8,128)(2,1)S(1)} %slice.158), channel_id=1, source_target_pairs={{1,0},{2,1},{3,2},{4,3},{5,4},{6,5},{7,6},{0,7},{9,8},{10,9},{11,1... | collective-permute-start | bytes 393224 | tf_op jit(solution)/shard_map/cond/branch_0_fun/ppermute | solution.py:46
  60.4 10.2 %collective-permute-start.23 = (bf16[512,768]{1,0:T(8,128)(2,1)S(1)}, bf16[512,768]{1,0:T(8,128)(2,1)S(1)}, u32[]{:S(2)}, u32[]{:S(2)}) collective-permute-start(bf16[512,768]{1,0:T(8,128)(2,1)S(1)} %get-tuple-element.67), channel_id=1, source_target_pairs={{0,8},{8,0},{1,9},{9,1},{2,10},{10,2},{3,11},{11,3},{4,12},{12,4},... | collective-permute-start | bytes 2359304 | tf_op jit(solution)/shard_map/cond/branch_0_fun/ppermute | solution.py:42
  63.9 6.5 %collective-permute-start.28 = (bf16[64,1024]{1,0:T(8,128)(2,1)S(1)}, bf16[64,1024]{1,0:T(8,128)(2,1)S(1)}, u32[]{:S(2)}, u32[]{:S(2)}) collective-permute-start(bf16[64,1024]{1,0:T(8,128)(2,1)S(1)} %slice.295), channel_id=1, source_target_pairs={{0,1},{1,0},{2,3},{3,2},{4,5},{5,4},{6,7},{7,6},{8,10},{9,11},{10,... | collective-permute-start | bytes 393224 | tf_op jit(solution)/shard_map/cond/branch_0_fun/ppermute | solution.py:38
  64.1 13.9 %collective-permute-start.18 = (bf16[256,768]{1,0:T(8,128)(2,1)S(1)}, bf16[256,768]{1,0:T(8,128)(2,1)S(1)}, u32[]{:S(2)}, u32[]{:S(2)}) collective-permute-start(bf16[256,768]{1,0:T(8,128)(2,1)S(1)} %slice.291), channel_id=1, source_target_pairs={{0,2},{1,3},{2,0},{3,1},{4,6},{5,7},{6,4},{7,5},{8,9},{9,8},{10,11... | collective-permute-start | bytes 1179656 | tf_op jit(solution)/shard_map/cond/branch_0_fun/ppermute | solution.py:38
  65.5 26.6 %collective-permute-start.20 = (bf16[128,1024]{1,0:T(8,128)(2,1)S(1)}, bf16[128,1024]{1,0:T(8,128)(2,1)S(1)}, u32[]{:S(2)}, u32[]{:S(2)}) collective-permute-start(bf16[128,1024]{1,0:T(8,128)(2,1)S(1)} %slice.216), channel_id=1, source_target_pairs={{1,0},{2,1},{3,2},{4,3},{5,4},{6,5},{7,6},{0,7},{9,8},{10,9},{11,1... | collective-permute-start | bytes 786440 | tf_op jit(solution)/shard_map/cond/branch_0_fun/ppermute | solution.py:46
  70.4 6.9 %collective-permute-start.29 = (bf16[32,1024]{1,0:T(8,128)(2,1)S(1)}, bf16[32,1024]{1,0:T(8,128)(2,1)S(1)}, u32[]{:S(2)}, u32[]{:S(2)}) collective-permute-start(bf16[32,1024]{1,0:T(8,128)(2,1)S(1)} %slice.298), channel_id=1, source_target_pairs={{0,4},{1,5},{2,6},{3,7},{4,0},{5,1},{6,2},{7,3},{8,12},{9,13},{10,... | collective-permute-start | bytes 196616 | tf_op jit(solution)/shard_map/cond/branch_0_fun/ppermute | solution.py:38
  70.8 15.3 %collective-permute-start.24 = (bf16[256,768]{1,0:T(8,128)(2,1)S(1)}, bf16[256,768]{1,0:T(8,128)(2,1)S(1)}, u32[]{:S(2)}, u32[]{:S(2)}) collective-permute-start(bf16[256,768]{1,0:T(8,128)(2,1)S(1)} %slice.290), channel_id=1, source_target_pairs={{0,2},{1,3},{2,0},{3,1},{4,6},{5,7},{6,4},{7,5},{8,9},{9,8},{10,11... | collective-permute-start | bytes 1179656 | tf_op jit(solution)/shard_map/cond/branch_0_fun/ppermute | solution.py:38
  78.1 8.2 %collective-permute-start.21 = (bf16[128,768]{1,0:T(8,128)(2,1)S(1)}, bf16[128,768]{1,0:T(8,128)(2,1)S(1)}, u32[]{:S(2)}, u32[]{:S(2)}) collective-permute-start(bf16[128,768]{1,0:T(8,128)(2,1)S(1)} %slice.294), channel_id=1, source_target_pairs={{0,1},{1,0},{2,3},{3,2},{4,5},{5,4},{6,7},{7,6},{8,10},{9,11},{10,... | collective-permute-start | bytes 589832 | tf_op jit(solution)/shard_map/cond/branch_0_fun/ppermute | solution.py:38
  86.2 5.7 %collective-permute-start.25 = (bf16[128,768]{1,0:T(8,128)(2,1)S(1)}, bf16[128,768]{1,0:T(8,128)(2,1)S(1)}, u32[]{:S(2)}, u32[]{:S(2)}) collective-permute-start(bf16[128,768]{1,0:T(8,128)(2,1)S(1)} %slice.293), channel_id=1, source_target_pairs={{0,1},{1,0},{2,3},{3,2},{4,5},{5,4},{6,7},{7,6},{8,10},{9,11},{10,... | collective-permute-start | bytes 589832 | tf_op jit(solution)/shard_map/cond/branch_0_fun/ppermute | solution.py:38
  86.4 8.5 %collective-permute-start.22 = (bf16[64,768]{1,0:T(8,128)(2,1)S(1)}, bf16[64,768]{1,0:T(8,128)(2,1)S(1)}, u32[]{:S(2)}, u32[]{:S(2)}) collective-permute-start(bf16[64,768]{1,0:T(8,128)(2,1)S(1)} %slice.297), channel_id=1, source_target_pairs={{0,4},{1,5},{2,6},{3,7},{4,0},{5,1},{6,2},{7,3},{8,12},{9,13},{10,... | collective-permute-start | bytes 294920 | tf_op jit(solution)/shard_map/cond/branch_0_fun/ppermute | solution.py:38
  92.0 5.6 %collective-permute-start.26 = (bf16[64,768]{1,0:T(8,128)(2,1)S(1)}, bf16[64,768]{1,0:T(8,128)(2,1)S(1)}, u32[]{:S(2)}, u32[]{:S(2)}) collective-permute-start(bf16[64,768]{1,0:T(8,128)(2,1)S(1)} %slice.296), channel_id=1, source_target_pairs={{0,4},{1,5},{2,6},{3,7},{4,0},{5,1},{6,2},{7,3},{8,12},{9,13},{10,... | collective-permute-start | bytes 294920 | tf_op jit(solution)/shard_map/cond/branch_0_fun/ppermute | solution.py:38
  (4 other events, 33.3 us)

commit v2 on v1

--- a/solution.py
+++ b/solution.py
@@ -370,7 +370,7 @@
     kept_out, last_out, _, _ = scatter_from(keep_out, swapped_out, rows)
     grad_out = kept_out + last_out.astype(F32)
     kept_a, last_a, first_a, seen_a = scatter_from(keep_a, swapped_a, rows)
-    kept_b, last_b, _, _ = scatter_from(keep_b, swapped_b, rows)
+    kept_b, last_b, _, seen_b = scatter_from(keep_b, swapped_b, rows)
     (grad_in,) = call(
         finish_kernel,
         [((dim // blocks, 3 * hidden), F32)],
@@ -386,8 +386,8 @@
         flops=2 * cells * dim * 3 * hidden,
         moved=6 << 20,
         name="grad",
-    )(xw, mean, inv, gp_a, after(gp_b, first_a), full_in, cot)
-    back_grad = shifted(part(grad_win), rows, -distance)
+    )(xw, mean, inv, gp_a, after(gp_b, first_a, back_ctx), full_in, cot)
+    back_grad = shifted(after(part(grad_win), seen_b[0]), rows, -distance)
     (output,) = call(
         functools.partial(output_kernel, **shape_kw),
         [((cells, dim), BF16)],

time: 98.2 us -> 96.7 us (0.985); the launches traced: 98.4 us -> 94.9 us
  waiting for transfers between devices: 48.4 us -> 40.6 us
  starting transfers between devices: 22.8 us -> 26.9 us
    ppermute x16, waiting for transfers between devices: 48.3 us -> 35.2 us  [exchange(): return lax.ppermute(block, ('fsdp', 'rows'), pairs)]
    ppermute x16, starting transfers between devices: 13.8 us -> 23.2 us  [exchange(): return lax.ppermute(block, ('fsdp', 'rows'), pairs)]
    ppermute x3, waiting for transfers between devices: 0.01 us -> 5.39 us  [shifted(): lax.ppermute(block, 'rows', [((i - distance) % rows, i) for i in range(ro...]
    ppermute x3, starting transfers between devices: 4.58 us -> 1.45 us  [shifted(): lax.ppermute(block, 'rows', [((i - distance) % rows, i) for i in range(ro...]
    ppermute x11, starting transfers between devices: 4.5 us -> 2.23 us  [swap_cores(): return lax.ppermute(block, 'fsdp', [(0, 1), (1, 0)])]
  transfers between devices with their start and end apart: 30 -> 30, of which waited for: 9 -> 13; matrix products, arithmetic and copies ran while one was open for 9% -> 10% of each run, Pallas kernels for 10% -> 10%
where the time goes in v2:
time: 96.7 us; the launch traced here: 94.9 us
  waiting for transfers between devices  40.6 us (42%)
  starting transfers between devices  26.9 us (28%)
  Pallas kernels  14.6 us (15%)
  other arithmetic  7.01 us (7%)
  local copies, waits for them, and re-layouts  3.84 us (4%)
  between operations  1.28 us (1%)
    ppermute x16, waiting for transfers between devices, exchange(): return lax.ppermute(block, ('fsdp', 'rows'), pairs)  35.2 us
    ppermute x16, starting transfers between devices, exchange(): return lax.ppermute(block, ('fsdp', 'rows'), pairs)  23.2 us
    ppermute x3, waiting for transfers between devices, shifted(): lax.ppermute(block, 'rows', [((i - distance) % rows, i) for i in range(ro...  5.39 us
    pallas_call x1, Pallas kernels, branch(): call(functools.partial(forward_kernel, blocks=blocks), [((dim, 3 * hidden...  3.2 us
    pallas_call x1, Pallas kernels, branch(): call(backward_a_kernel, [((cells, hidden), BF16)] + half_outs, [VM] * 5,...  2.62 us
    ppermute x11, starting transfers between devices, swap_cores(): return lax.ppermute(block, 'fsdp', [(0, 1), (1, 0)])  2.23 us
    pallas_call x1, Pallas kernels, branch(): call(backward_b_kernel, half_outs, [VM, VM, VM, VM], flops=4 * cells * di...  2.21 us
    slice x5, local copies, waits for them, and re-layouts, branch(): part = lambda a: lax.slice_in_dim(a, low, low + half, axis=0)  1.97 us
  transfers between devices with their start and end apart: 30, of which 13 were waited for; matrix products, arithmetic and copies ran while one was open for 10% of the time, Pallas kernels for 10%

profile of v2, /device:TPU:0, one launch (start us, length us, event | category | flops | bytes accessed | tf_op | source)
XLA Modules:
  0.0 94.9 jit_solution(969064311141183628)
XLA Ops:
  1.3 93.6 %conditional.1 = (bf16[1,16,16,1024]{3,2,1,0:T(8,128)(2,1)}, bf16[1,16,16,1024]{3,2,1,0:T(8,128)(2,1)}, f32[64,1536]{1,0:T(8,128)}, f32[32,1024]{1,0:T(8,128)}) conditional(s32[]{:T(128)} %bitcast.18, (bf16[1,16,16,1024]{3,2,1,0:T(8,128)(2,1)}, s32[8]{0:T(128)}, s32[8]{0:T(128)}, s32[1,16,16]{2,1,0:T(8,128)}, bf16[1,16,16,1024]{3,2,1,0:T(8,128)(2,1)}, ...), branch_computations={%region_0.1_spmd, %region_1.2_spmd} | conditional | flops 6992472064 | bytes 108641328 | solution.py:406
  3.3 4.1 %collective-permute-start.31 = (bf16[64,2048]{1,0:T(8,128)(2,1)S(1)}, bf16[64,2048]{1,0:T(8,128)(2,1)S(1)}, u32[]{:S(2)}, u32[]{:S(2)}) collective-permute-start(bf16[64,2048]{1,0:T(8,128)(2,1)S(1)} %maximum_maximum_fusion.1.refs_0_), channel_id=1, source_target_pairs={{0,4},{1,5},{2,6},{3,7},{4,0},{5,1},{6,2},{7,3},{8,12},{9,13},{10,... | collective-permute-start | bytes 786440 | tf_op jit(solution)/shard_map/cond/branch_1_fun/ppermute | solution.py:38
  7.4 1.5 %collective-permute-start.32 = (bf16[64,2048]{1,0:T(8,128)(2,1)S(1)}, bf16[64,2048]{1,0:T(8,128)(2,1)S(1)}, u32[]{:S(2)}, u32[]{:S(2)}) collective-permute-start(bf16[64,2048]{1,0:T(8,128)(2,1)S(1)} %maximum_maximum_fusion.1.refs_0_), channel_id=1, source_target_pairs={{0,1},{1,0},{2,3},{3,2},{4,5},{5,4},{6,7},{7,6},{8,10},{9,11},{10,... | collective-permute-start | bytes 786440 | tf_op jit(solution)/shard_map/cond/branch_1_fun/ppermute | solution.py:38
  8.9 1.6 %collective-permute-start.34 = (bf16[64,2048]{1,0:T(8,128)(2,1)S(1)}, bf16[64,2048]{1,0:T(8,128)(2,1)S(1)}, u32[]{:S(2)}, u32[]{:S(2)}) collective-permute-start(bf16[64,2048]{1,0:T(8,128)(2,1)S(1)} %maximum_maximum_fusion.1.refs_0_), channel_id=1, source_target_pairs={{0,2},{1,3},{2,0},{3,1},{4,6},{5,7},{6,4},{7,5},{8,9},{9,8},{10,11... | collective-permute-start | bytes 786440 | tf_op jit(solution)/shard_map/cond/branch_1_fun/ppermute | solution.py:38
  11.5 1.0 %slice.182 = bf16[1,8,16,1024]{3,2,1,0:T(8,128)(2,1)S(1)} slice(bf16[1,16,16,1024]{3,2,1,0:T(8,128)(2,1)} %get-tuple-element.75), slice={[0:1], [0:8], [0:16], [0:1024]} | slice | bytes 524288 | tf_op jit(solution)/shard_map/cond/branch_1_fun/slice | solution.py:293
  14.0 6.2 %collective-permute-done.31.refs_1_ = bf16[64,2048]{1,0:T(8,128)(2,1)S(1)} collective-permute-done((bf16[64,2048]{1,0:T(8,128)(2,1)S(1)}, bf16[64,2048]{1,0:T(8,128)(2,1)S(1)}, u32[]{:S(2)}, u32[]{:S(2)}) %collective-permute-start.31) | collective-permute-done | bytes 262176 | tf_op jit(solution)/shard_map/cond/branch_1_fun/ppermute | solution.py:38
  21.0 1.2 %collective-permute-start.35 = (bf16[64,2048]{1,0:T(8,128)(2,1)S(1)}, bf16[64,2048]{1,0:T(8,128)(2,1)S(1)}, u32[]{:S(2)}, u32[]{:S(2)}) collective-permute-start(bf16[64,2048]{1,0:T(8,128)(2,1)S(1)} %collective-permute-done.31.refs_1_), channel_id=1, source_target_pairs={{0,2},{1,3},{2,0},{3,1},{4,6},{5,7},{6,4},{7,5},{8,9},{9,8},{10,11... | collective-permute-start | bytes 786440 | tf_op jit(solution)/shard_map/cond/branch_1_fun/ppermute | solution.py:38
  22.3 1.3 %fusion.23 = s32[256]{0:T(256)S(1)} fusion(pred[]{:T(512)S(6)} %eq.45, s32[]{:T(128)} %bitcast.13, s32[]{:T(128)} %bitcast.12), kind=kLoop, calls=%fused_computation.92 | loop fusion | flops 4608 | bytes 1033 | tf_op jit(solution)/shard_map/cond/branch_1_fun/add | solution.py:313
  24.5 11.9 %collective-permute-done.33.refs_3_ = bf16[64,2048]{1,0:T(8,128)(2,1)S(1)} collective-permute-done((bf16[64,2048]{1,0:T(8,128)(2,1)S(1)}, bf16[64,2048]{1,0:T(8,128)(2,1)S(1)}, u32[]{:S(2)}, u32[]{:S(2)}) %collective-permute-start.33) | collective-permute-done | bytes 262176 | tf_op jit(solution)/shard_map/cond/branch_1_fun/ppermute | solution.py:38
  37.4 1.3 %collective-permute-start.37 = (bf16[64,2048]{1,0:T(8,128)(2,1)S(1)}, bf16[64,2048]{1,0:T(8,128)(2,1)S(1)}, u32[]{:S(2)}, u32[]{:S(2)}) collective-permute-start(bf16[64,2048]{1,0:T(8,128)(2,1)S(1)} %collective-permute-done.33.refs_3_), channel_id=1, source_target_pairs={{0,2},{1,3},{2,0},{3,1},{4,6},{5,7},{6,4},{7,5},{8,9},{9,8},{10,11... | collective-permute-start | bytes 786440 | tf_op jit(solution)/shard_map/cond/branch_1_fun/ppermute | solution.py:38
  40.8 3.0 %collective-permute-done.37.refs_7_ = bf16[64,2048]{1,0:T(8,128)(2,1)S(1)} collective-permute-done((bf16[64,2048]{1,0:T(8,128)(2,1)S(1)}, bf16[64,2048]{1,0:T(8,128)(2,1)S(1)}, u32[]{:S(2)}, u32[]{:S(2)}) %collective-permute-start.37) | collective-permute-done | bytes 262176 | tf_op jit(solution)/shard_map/cond/branch_1_fun/ppermute | solution.py:38
  44.4 1.7 %norm.3 = (bf16[256,1024]{1,0:T(8,128)(2,1)S(1)}, bf16[256,1024]{1,0:T(8,128)(2,1)S(1)}, bf16[1024,256]{1,0:T(8,128)(2,1)S(1)}, f32[256,1]{1,0:T(8,128)S(1)}, f32[256,1]{1,0:T(8,128)S(1)}) custom-call(s32[2]{0:T(128)S(1)} %copy-done.5, s32[16]{0:T(128)S(1)} %pad_add_fusion.1.table.place_at.order, bf16[256,1024]{1,0:T(8,128)(2,1)} %bitcast.24, ...), custom_call_target="tpu_custom_call" | custom-call | flops 5242880 | bytes 2621440 | tf_op jit(solution)/shard_map/cond/branch_1_fun/norm/pallas_call | solution.py:322
  46.3 3.2 %fwd.3 = (bf16[1024,1536]{1,0:T(8,128)(2,1)S(1)}, bf16[512,1024]{1,0:T(8,128)(2,1)S(1)}, bf16[256,1536]{1,0:T(8,128)(2,1)S(1)}, f32[8,256,256]{2,1,0:T(8,128)S(1...) custom-call(s32[16]{0:T(128)S(1)} %pad_add_fusion.1.table.place_at.order, ...), custom_call_target="tpu_custom_call" | custom-call | flops 2415919104 | bytes 10485760 | tf_op jit(solution)/shard_map/cond/branch_1_fun/fwd/pallas_call | solution.py:331
  49.5 1.0 %term_out.3 = (bf16[256,1024]{1,0:T(8,128)(2,1)S(1)}, f32[256,1024]{1,0:T(8,128)S(1)}, bf16[256,1024]{1,0:T(8,128)(2,1)S(1)}) custom-call(s32[2]{0:T(128)S(1)} %copy-done.5, bf16[512,256]{1,0:T(8,128)(2,1)S(1)} %get-tuple-element.84.ctx_ordered, bf16[256,1024]{1,0:T(8,128)(2,1)S(1)} %bitcast.27, bf16[128,1024]{1,0:T(8,128)(2,1)S(1)} %slice.236.halo), custom_call_target="tpu_custom_call" | custom-call | flops 268435456 | bytes 4194304 | tf_op jit(solution)/shard_map/cond/branch_1_fun/term_out/pallas_call | solution.py:340
  51.1 2.6 %bwd_a.3 = (bf16[256,512]{1,0:T(8,128)(2,1)S(1)}, bf16[256,768]{1,0:T(8,128)(2,1)S(1)}, f32[512,768]{1,0:T(8,128)S(1)}, bf16[512,768]{1,0:T(8,128)(2,1)S(1)}) custom-call(bf16[256,1024]{1,0:T(8,128)(2,1)S(1)} %get-tuple-element.85.cot, bf16[256,1536]{1,0:T(8,128)(2,1)S(1)} %get-tuple-element.86.packed, f32[8,256,256]{2,1,0:T(8,128)S(1)} %get-tuple-element.87.attn, ...), custom_call_target="tpu_custom_call" | custom-call | flops 1610612736 | bytes 6291456 | tf_op jit(solution)/shard_map/cond/branch_1_fun/bwd_a/pallas_call | solution.py:351
  54.1 1.4 %collective-permute-start.57 = (bf16[128,1024]{1,0:T(8,128)(2,1)S(1)}, bf16[128,1024]{1,0:T(8,128)(2,1)S(1)}, u32[]{:S(2)}, u32[]{:S(2)}) collective-permute-start(bf16[128,1024]{1,0:T(8,128)(2,1)S(1)} %slice.301), channel_id=1, source_target_pairs={{0,2},{1,3},{2,0},{3,1},{4,6},{5,7},{6,4},{7,5},{8,9},{9,8},{10,11... | collective-permute-start | bytes 786440 | tf_op jit(solution)/shard_map/cond/branch_1_fun/ppermute | solution.py:38
  56.1 1.2 %collective-permute-start.46 = (bf16[128,512]{1,0:T(8,128)(2,1)S(1)}, bf16[128,512]{1,0:T(8,128)(2,1)S(1)}, u32[]{:S(2)}, u32[]{:S(2)}) collective-permute-start(bf16[128,512]{1,0:T(8,128)(2,1)S(1)} %slice.189), channel_id=1, source_target_pairs={{7,0},{0,1},{1,2},{2,3},{3,4},{4,5},{5,6},{6,7},{15,8},{8,9},{9,10... | collective-permute-start | bytes 393224 | tf_op jit(solution)/shard_map/cond/branch_1_fun/ppermute | solution.py:46
  57.3 2.2 %bwd_b.3 = (bf16[256,768]{1,0:T(8,128)(2,1)S(1)}, f32[512,768]{1,0:T(8,128)S(1)}, bf16[512,768]{1,0:T(8,128)(2,1)S(1)}) custom-call(bf16[256,1536]{1,0:T(8,128)(2,1)S(1)} %get-tuple-element.86.packed, f32[8,256,256]{2,1,0:T(8,128)S(1)} %get-tuple-element.87.attn, bf16[256,512]{1,0:T(8,128)(2,1)S(1)} %get-tuple-element.100.gctx, ...), custom_call_target="tpu_custom_call" | custom-call | flops 1610612736 | bytes 6291456 | tf_op jit(solution)/shard_map/cond/branch_1_fun/bwd_b/pallas_call | solution.py:361
  60.6 2.0 %collective-permute-start.58 = (bf16[64,1024]{1,0:T(8,128)(2,1)S(1)}, bf16[64,1024]{1,0:T(8,128)(2,1)S(1)}, u32[]{:S(2)}, u32[]{:S(2)}) collective-permute-start(bf16[64,1024]{1,0:T(8,128)(2,1)S(1)} %slice.304), channel_id=1, source_target_pairs={{0,1},{1,0},{2,3},{3,2},{4,5},{5,4},{6,7},{7,6},{8,10},{9,11},{10,... | collective-permute-start | bytes 393224 | tf_op jit(solution)/shard_map/cond/branch_1_fun/ppermute | solution.py:38
  62.8 1.3 %collective-permute-start.48 = (bf16[256,768]{1,0:T(8,128)(2,1)S(1)}, bf16[256,768]{1,0:T(8,128)(2,1)S(1)}, u32[]{:S(2)}, u32[]{:S(2)}) collective-permute-start(bf16[256,768]{1,0:T(8,128)(2,1)S(1)} %slice.300), channel_id=1, source_target_pairs={{0,2},{1,3},{2,0},{3,1},{4,6},{5,7},{6,4},{7,5},{8,9},{9,8},{10,11... | collective-permute-start | bytes 1179656 | tf_op jit(solution)/shard_map/cond/branch_1_fun/ppermute | solution.py:38
  64.2 1.8 %collective-permute-done.46.back = bf16[128,512]{1,0:T(8,128)(2,1)S(1)} collective-permute-done((bf16[128,512]{1,0:T(8,128)(2,1)S(1)}, bf16[128,512]{1,0:T(8,128)(2,1)S(1)}, u32[]{:S(2)}, u32[]{:S(2)}) %collective-permute-start.46) | collective-permute-done | bytes 131104 | tf_op jit(solution)/shard_map/cond/branch_1_fun/ppermute | solution.py:46
  66.0 1.3 %grad.3 = bf16[256,1024]{1,0:T(8,128)(2,1)S(1)} custom-call(bf16[256,1024]{1,0:T(8,128)(2,1)S(1)} %get-tuple-element.95.xw, f32[256,1]{1,0:T(8,128)S(1)} %get-tuple-element.96.mean, f32[256,1]{1,0:T(8,128)S(1)} %get-tuple-element.97.inv, bf16[256,768]{1,0:T(8,128)(2,1)S(1)} %get-tuple-element.90.gp_a, bf16[256,768]{1,0:T(8,128)(2,1)S(1)} %get-tuple-element.102.gp_b, ...), custom_call_target="tpu_custom_call" | custom-call | flops 805306368 | bytes 6291456 | tf_op jit(solution)/shard_map/cond/branch_1_fun/grad/pallas_call | solution.py:381
  67.3 1.3 %collective-permute-done.58 = bf16[64,1024]{1,0:T(8,128)(2,1)S(1)} collective-permute-done((bf16[64,1024]{1,0:T(8,128)(2,1)S(1)}, bf16[64,1024]{1,0:T(8,128)(2,1)S(1)}, u32[]{:S(2)}, u32[]{:S(2)}) %collective-permute-start.58) | collective-permute-done | bytes 131104 | tf_op jit(solution)/shard_map/cond/branch_1_fun/ppermute | solution.py:38
  69.4 2.7 %collective-permute-start.51 = (bf16[256,768]{1,0:T(8,128)(2,1)S(1)}, bf16[256,768]{1,0:T(8,128)(2,1)S(1)}, u32[]{:S(2)}, u32[]{:S(2)}) collective-permute-start(bf16[256,768]{1,0:T(8,128)(2,1)S(1)} %slice.299), channel_id=1, source_target_pairs={{0,2},{1,3},{2,0},{3,1},{4,6},{5,7},{6,4},{7,5},{8,9},{9,8},{10,11... | collective-permute-start | bytes 1179656 | tf_op jit(solution)/shard_map/cond/branch_1_fun/ppermute | solution.py:38
  72.1 2.6 %collective-permute-done.59 = bf16[32,1024]{1,0:T(8,128)(2,1)S(1)} collective-permute-done((bf16[32,1024]{1,0:T(8,128)(2,1)S(1)}, bf16[32,1024]{1,0:T(8,128)(2,1)S(1)}, u32[]{:S(2)}, u32[]{:S(2)}) %collective-permute-start.59) | collective-permute-done | bytes 65568 | tf_op jit(solution)/shard_map/cond/branch_1_fun/ppermute | solution.py:38
  75.6 1.8 %output.3 = bf16[256,1024]{1,0:T(8,128)(2,1)} custom-call(s32[2]{0:T(128)S(1)} %copy-done.5, bf16[256,1024]{1,0:T(8,128)(2,1)S(1)} %bitcast.25, bf16[256,512]{1,0:T(8,128)(2,1)S(1)} %get-tuple-element.83.ctx, bf16[128,512]{1,0:T(8,128)(2,1)S(1)} %collective-permute-done.46.back, bf16[512,1024]{1,0:T(8,128)(2,1)S(1)} %get-tuple-element.89.full), custom_call_target="tpu_custom_call" | custom-call | flops 268435456 | bytes 3145728 | tf_op jit(solution)/shard_map/cond/branch_1_fun/output/pallas_call | solution.py:391
  77.4 4.2 %collective-permute-done.51 = bf16[256,768]{1,0:T(8,128)(2,1)S(1)} collective-permute-done((bf16[256,768]{1,0:T(8,128)(2,1)S(1)}, bf16[256,768]{1,0:T(8,128)(2,1)S(1)}, u32[]{:S(2)}, u32[]{:S(2)}) %collective-permute-start.51) | collective-permute-done | bytes 393248 | tf_op jit(solution)/shard_map/cond/branch_1_fun/ppermute | solution.py:38
  81.7 1.8 %collective-permute-start.55 = (bf16[128,768]{1,0:T(8,128)(2,1)S(1)}, bf16[128,768]{1,0:T(8,128)(2,1)S(1)}, u32[]{:S(2)}, u32[]{:S(2)}) collective-permute-start(bf16[128,768]{1,0:T(8,128)(2,1)S(1)} %slice.302), channel_id=1, source_target_pairs={{0,1},{1,0},{2,3},{3,2},{4,5},{5,4},{6,7},{7,6},{8,10},{9,11},{10,... | collective-permute-start | bytes 589832 | tf_op jit(solution)/shard_map/cond/branch_1_fun/ppermute | solution.py:38
  83.9 1.3 %collective-permute-start.54 = (bf16[64,768]{1,0:T(8,128)(2,1)S(1)}, bf16[64,768]{1,0:T(8,128)(2,1)S(1)}, u32[]{:S(2)}, u32[]{:S(2)}) collective-permute-start(bf16[64,768]{1,0:T(8,128)(2,1)S(1)} %slice.306), channel_id=1, source_target_pairs={{0,4},{1,5},{2,6},{3,7},{4,0},{5,1},{6,2},{7,3},{8,12},{9,13},{10,... | collective-permute-start | bytes 294920 | tf_op jit(solution)/shard_map/cond/branch_1_fun/ppermute | solution.py:38
  85.2 3.3 %collective-permute-done.55 = bf16[128,768]{1,0:T(8,128)(2,1)S(1)} collective-permute-done((bf16[128,768]{1,0:T(8,128)(2,1)S(1)}, bf16[128,768]{1,0:T(8,128)(2,1)S(1)}, u32[]{:S(2)}, u32[]{:S(2)}) %collective-permute-start.55) | collective-permute-done | bytes 196640 | tf_op jit(solution)/shard_map/cond/branch_1_fun/ppermute | solution.py:38
  89.1 3.5 %collective-permute-done.52 = bf16[128,1024]{1,0:T(8,128)(2,1)S(1)} collective-permute-done((bf16[128,1024]{1,0:T(8,128)(2,1)S(1)}, bf16[128,1024]{1,0:T(8,128)(2,1)S(1)}, u32[]{:S(2)}, u32[]{:S(2)}) %collective-permute-start.52) | collective-permute-done | bytes 262176 | tf_op jit(solution)/shard_map/cond/branch_1_fun/ppermute | solution.py:46
  92.7 1.0 %pad_select_fusion.1 = bf16[256,1024]{1,0:T(8,128)(2,1)} fusion(bf16[256,1024]{1,0:T(8,128)(2,1)S(1)} %grad.3, bf16[128,1024]{1,0:T(8,128)(2,1)S(1)} %collective-permute-done.52, pred[256]{0:T(512)(128)(4,1)S(1)} %fusion.24), kind=kLoop, calls=%fused_computation.67 | loop fusion | flops 262144 | bytes 1310976 | tf_op jit(solution)/shard_map/cond/branch_1_fun/jit(_where)/select_n | solution.py:400
  (92 shorter events, 16.4 us)
Async XLA Ops:
  1.5 22.0 %copy-start.9 = (s32[8]{0:T(128)S(1)}, s32[8]{0:T(128)}, u32[]{:S(2)}) copy-start(s32[8]{0:T(128)} %get-tuple-element.72) | copy-start | bytes 100 | tf_op jit(solution)/shard_map/cond
  1.6 22.0 %copy-start.11 = (s32[8]{0:T(128)S(1)}, s32[8]{0:T(128)}, u32[]{:S(2)}) copy-start(s32[8]{0:T(128)} %get-tuple-element.73) | copy-start | bytes 100 | tf_op jit(solution)/shard_map/cond
  3.3 16.9 %collective-permute-start.31 = (bf16[64,2048]{1,0:T(8,128)(2,1)S(1)}, bf16[64,2048]{1,0:T(8,128)(2,1)S(1)}, u32[]{:S(2)}, u32[]{:S(2)}) collective-permute-start(bf16[64,2048]{1,0:T(8,128)(2,1)S(1)} %maximum_maximum_fusion.1.refs_0_), channel_id=1, source_target_pairs={{0,4},{1,5},{2,6},{3,7},{4,0},{5,1},{6,2},{7,3},{8,12},{9,13},{10,... | collective-permute-start | bytes 786440 | tf_op jit(solution)/shard_map/cond/branch_1_fun/ppermute | solution.py:38
  7.4 12.8 %collective-permute-start.32 = (bf16[64,2048]{1,0:T(8,128)(2,1)S(1)}, bf16[64,2048]{1,0:T(8,128)(2,1)S(1)}, u32[]{:S(2)}, u32[]{:S(2)}) collective-permute-start(bf16[64,2048]{1,0:T(8,128)(2,1)S(1)} %maximum_maximum_fusion.1.refs_0_), channel_id=1, source_target_pairs={{0,1},{1,0},{2,3},{3,2},{4,5},{5,4},{6,7},{7,6},{8,10},{9,11},{10,... | collective-permute-start | bytes 786440 | tf_op jit(solution)/shard_map/cond/branch_1_fun/ppermute | solution.py:38
  8.9 12.1 %collective-permute-start.34 = (bf16[64,2048]{1,0:T(8,128)(2,1)S(1)}, bf16[64,2048]{1,0:T(8,128)(2,1)S(1)}, u32[]{:S(2)}, u32[]{:S(2)}) collective-permute-start(bf16[64,2048]{1,0:T(8,128)(2,1)S(1)} %maximum_maximum_fusion.1.refs_0_), channel_id=1, source_target_pairs={{0,2},{1,3},{2,0},{3,1},{4,6},{5,7},{6,4},{7,5},{8,9},{9,8},{10,11... | collective-permute-start | bytes 786440 | tf_op jit(solution)/shard_map/cond/branch_1_fun/ppermute | solution.py:38
  13.4 23.9 %collective-permute-start.30 = (bf16[272,1024]{1,0:T(8,128)(2,1)}, bf16[272,1024]{1,0:T(8,128)(2,1)S(1)}, u32[]{:S(2)}, u32[]{:S(2)}) collective-permute-start(bf16[272,1024]{1,0:T(8,128)(2,1)} %fusion.17), channel_id=1, source_target_pairs={{1,0},{2,1},{3,2},{4,3},{5,4},{6,5},{7,6},{0,7},{9,8},{10,9},{11,1... | collective-permute-start | bytes 1671176 | tf_op jit(solution)/shard_map/cond/branch_1_fun/ppermute | solution.py:46
  13.4 25.4 %collective-permute-start.38 = (bf16[64,2048]{1,0:T(8,128)(2,1)S(1)}, bf16[64,2048]{1,0:T(8,128)(2,1)S(1)}, u32[]{:S(2)}, u32[]{:S(2)}) collective-permute-start(bf16[64,2048]{1,0:T(8,128)(2,1)S(1)} %maximum_maximum_fusion.1.refs_0_), channel_id=1, source_target_pairs={{0,8},{8,0},{1,9},{9,1},{2,10},{10,2},{3,11},{11,3},{4,12},{12,4},... | collective-permute-start | bytes 786440 | tf_op jit(solution)/shard_map/cond/branch_1_fun/ppermute | solution.py:42
  20.2 16.1 %collective-permute-start.33 = (bf16[64,2048]{1,0:T(8,128)(2,1)S(1)}, bf16[64,2048]{1,0:T(8,128)(2,1)S(1)}, u32[]{:S(2)}, u32[]{:S(2)}) collective-permute-start(bf16[64,2048]{1,0:T(8,128)(2,1)S(1)} %collective-permute-done.31.refs_1_), channel_id=1, source_target_pairs={{0,1},{1,0},{2,3},{3,2},{4,5},{5,4},{6,7},{7,6},{8,10},{9,11},{10,... | collective-permute-start | bytes 786440 | tf_op jit(solution)/shard_map/cond/branch_1_fun/ppermute | solution.py:38
  21.0 16.3 %collective-permute-start.35 = (bf16[64,2048]{1,0:T(8,128)(2,1)S(1)}, bf16[64,2048]{1,0:T(8,128)(2,1)S(1)}, u32[]{:S(2)}, u32[]{:S(2)}) collective-permute-start(bf16[64,2048]{1,0:T(8,128)(2,1)S(1)} %collective-permute-done.31.refs_1_), channel_id=1, source_target_pairs={{0,2},{1,3},{2,0},{3,1},{4,6},{5,7},{6,4},{7,5},{8,9},{9,8},{10,11... | collective-permute-start | bytes 786440 | tf_op jit(solution)/shard_map/cond/branch_1_fun/ppermute | solution.py:38
  23.6 16.6 %collective-permute-start.36 = (bf16[64,2048]{1,0:T(8,128)(2,1)S(1)}, bf16[64,2048]{1,0:T(8,128)(2,1)S(1)}, u32[]{:S(2)}, u32[]{:S(2)}) collective-permute-start(bf16[64,2048]{1,0:T(8,128)(2,1)S(1)} %collective-permute-done.32.refs_2_), channel_id=1, source_target_pairs={{0,2},{1,3},{2,0},{3,1},{4,6},{5,7},{6,4},{7,5},{8,9},{9,8},{10,11... | collective-permute-start | bytes 786440 | tf_op jit(solution)/shard_map/cond/branch_1_fun/ppermute | solution.py:38
  36.4 3.8 %collective-permute-start.39 = (bf16[64,2048]{1,0:T(8,128)(2,1)S(1)}, bf16[64,2048]{1,0:T(8,128)(2,1)S(1)}, u32[]{:S(2)}, u32[]{:S(2)}) collective-permute-start(bf16[64,2048]{1,0:T(8,128)(2,1)S(1)} %collective-permute-done.31.refs_1_), channel_id=1, source_target_pairs={{0,8},{8,0},{1,9},{9,1},{2,10},{10,2},{3,11},{11,3},{4,12},{12,4},... | collective-permute-start | bytes 786440 | tf_op jit(solution)/shard_map/cond/branch_1_fun/ppermute | solution.py:42
  37.4 3.3 %collective-permute-start.40 = (bf16[64,2048]{1,0:T(8,128)(2,1)S(1)}, bf16[64,2048]{1,0:T(8,128)(2,1)S(1)}, u32[]{:S(2)}, u32[]{:S(2)}) collective-permute-start(bf16[64,2048]{1,0:T(8,128)(2,1)S(1)} %collective-permute-done.32.refs_2_), channel_id=1, source_target_pairs={{0,8},{8,0},{1,9},{9,1},{2,10},{10,2},{3,11},{11,3},{4,12},{12,4},... | collective-permute-start | bytes 786440 | tf_op jit(solution)/shard_map/cond/branch_1_fun/ppermute | solution.py:42
  37.4 6.4 %collective-permute-start.37 = (bf16[64,2048]{1,0:T(8,128)(2,1)S(1)}, bf16[64,2048]{1,0:T(8,128)(2,1)S(1)}, u32[]{:S(2)}, u32[]{:S(2)}) collective-permute-start(bf16[64,2048]{1,0:T(8,128)(2,1)S(1)} %collective-permute-done.33.refs_3_), channel_id=1, source_target_pairs={{0,2},{1,3},{2,0},{3,1},{4,6},{5,7},{6,4},{7,5},{8,9},{9,8},{10,11... | collective-permute-start | bytes 786440 | tf_op jit(solution)/shard_map/cond/branch_1_fun/ppermute | solution.py:38
  38.9 7.4 %collective-permute-start.42 = (bf16[64,2048]{1,0:T(8,128)(2,1)S(1)}, bf16[64,2048]{1,0:T(8,128)(2,1)S(1)}, u32[]{:S(2)}, u32[]{:S(2)}) collective-permute-start(bf16[64,2048]{1,0:T(8,128)(2,1)S(1)} %collective-permute-done.34.refs_4_), channel_id=1, source_target_pairs={{0,8},{8,0},{1,9},{9,1},{2,10},{10,2},{3,11},{11,3},{4,12},{12,4},... | collective-permute-start | bytes 786440 | tf_op jit(solution)/shard_map/cond/branch_1_fun/ppermute | solution.py:42
  40.2 6.1 %collective-permute-start.41 = (bf16[64,2048]{1,0:T(8,128)(2,1)S(1)}, bf16[64,2048]{1,0:T(8,128)(2,1)S(1)}, u32[]{:S(2)}, u32[]{:S(2)}) collective-permute-start(bf16[64,2048]{1,0:T(8,128)(2,1)S(1)} %collective-permute-done.33.refs_3_), channel_id=1, source_target_pairs={{0,8},{8,0},{1,9},{9,1},{2,10},{10,2},{3,11},{11,3},{4,12},{12,4},... | collective-permute-start | bytes 786440 | tf_op jit(solution)/shard_map/cond/branch_1_fun/ppermute | solution.py:42
  40.2 6.1 %collective-permute-start.43 = (bf16[64,2048]{1,0:T(8,128)(2,1)S(1)}, bf16[64,2048]{1,0:T(8,128)(2,1)S(1)}, u32[]{:S(2)}, u32[]{:S(2)}) collective-permute-start(bf16[64,2048]{1,0:T(8,128)(2,1)S(1)} %collective-permute-done.35.refs_5_), channel_id=1, source_target_pairs={{0,8},{8,0},{1,9},{9,1},{2,10},{10,2},{3,11},{11,3},{4,12},{12,4},... | collective-permute-start | bytes 786440 | tf_op jit(solution)/shard_map/cond/branch_1_fun/ppermute | solution.py:42
  40.7 5.6 %collective-permute-start.44 = (bf16[64,2048]{1,0:T(8,128)(2,1)S(1)}, bf16[64,2048]{1,0:T(8,128)(2,1)S(1)}, u32[]{:S(2)}, u32[]{:S(2)}) collective-permute-start(bf16[64,2048]{1,0:T(8,128)(2,1)S(1)} %collective-permute-done.36.refs_6_), channel_id=1, source_target_pairs={{0,8},{8,0},{1,9},{9,1},{2,10},{10,2},{3,11},{11,3},{4,12},{12,4},... | collective-permute-start | bytes 786440 | tf_op jit(solution)/shard_map/cond/branch_1_fun/ppermute | solution.py:42
  43.7 2.6 %collective-permute-start.45 = (bf16[64,2048]{1,0:T(8,128)(2,1)S(1)}, bf16[64,2048]{1,0:T(8,128)(2,1)S(1)}, u32[]{:S(2)}, u32[]{:S(2)}) collective-permute-start(bf16[64,2048]{1,0:T(8,128)(2,1)S(1)} %collective-permute-done.37.refs_7_), channel_id=1, source_target_pairs={{0,8},{8,0},{1,9},{9,1},{2,10},{10,2},{3,11},{11,3},{4,12},{12,4},... | collective-permute-start | bytes 786440 | tf_op jit(solution)/shard_map/cond/branch_1_fun/ppermute | solution.py:42
  50.6 3.3 %collective-permute-start.49 = (bf16[256,1024]{1,0:T(8,128)(2,1)S(1)}, bf16[256,1024]{1,0:T(8,128)(2,1)S(1)}, u32[]{:S(2)}, u32[]{:S(2)}) collective-permute-start(bf16[256,1024]{1,0:T(8,128)(2,1)S(1)} %get-tuple-element.99), channel_id=1, source_target_pairs={{0,8},{8,0},{1,9},{9,1},{2,10},{10,2},{3,11},{11,3},{4,12},{12,4},... | collective-permute-start | bytes 1572872 | tf_op jit(solution)/shard_map/cond/branch_1_fun/ppermute | solution.py:42
  53.8 8.9 %collective-permute-start.47 = (bf16[512,768]{1,0:T(8,128)(2,1)S(1)}, bf16[512,768]{1,0:T(8,128)(2,1)S(1)}, u32[]{:S(2)}, u32[]{:S(2)}) collective-permute-start(bf16[512,768]{1,0:T(8,128)(2,1)S(1)} %get-tuple-element.93), channel_id=1, source_target_pairs={{0,8},{8,0},{1,9},{9,1},{2,10},{10,2},{3,11},{11,3},{4,12},{12,4},... | collective-permute-start | bytes 2359304 | tf_op jit(solution)/shard_map/cond/branch_1_fun/ppermute | solution.py:42
  54.1 6.4 %collective-permute-start.57 = (bf16[128,1024]{1,0:T(8,128)(2,1)S(1)}, bf16[128,1024]{1,0:T(8,128)(2,1)S(1)}, u32[]{:S(2)}, u32[]{:S(2)}) collective-permute-start(bf16[128,1024]{1,0:T(8,128)(2,1)S(1)} %slice.301), channel_id=1, source_target_pairs={{0,2},{1,3},{2,0},{3,1},{4,6},{5,7},{6,4},{7,5},{8,9},{9,8},{10,11... | collective-permute-start | bytes 786440 | tf_op jit(solution)/shard_map/cond/branch_1_fun/ppermute | solution.py:38
  56.1 9.9 %collective-permute-start.46 = (bf16[128,512]{1,0:T(8,128)(2,1)S(1)}, bf16[128,512]{1,0:T(8,128)(2,1)S(1)}, u32[]{:S(2)}, u32[]{:S(2)}) collective-permute-start(bf16[128,512]{1,0:T(8,128)(2,1)S(1)} %slice.189), channel_id=1, source_target_pairs={{7,0},{0,1},{1,2},{2,3},{3,4},{4,5},{5,6},{6,7},{15,8},{8,9},{9,10... | collective-permute-start | bytes 393224 | tf_op jit(solution)/shard_map/cond/branch_1_fun/ppermute | solution.py:46
  59.5 9.6 %collective-permute-start.50 = (bf16[512,768]{1,0:T(8,128)(2,1)S(1)}, bf16[512,768]{1,0:T(8,128)(2,1)S(1)}, u32[]{:S(2)}, u32[]{:S(2)}) collective-permute-start(bf16[512,768]{1,0:T(8,128)(2,1)S(1)} %get-tuple-element.105), channel_id=1, source_target_pairs={{0,8},{8,0},{1,9},{9,1},{2,10},{10,2},{3,11},{11,3},{4,12},{12,4},... | collective-permute-start | bytes 2359304 | tf_op jit(solution)/shard_map/cond/branch_1_fun/ppermute | solution.py:42
  60.6 8.1 %collective-permute-start.58 = (bf16[64,1024]{1,0:T(8,128)(2,1)S(1)}, bf16[64,1024]{1,0:T(8,128)(2,1)S(1)}, u32[]{:S(2)}, u32[]{:S(2)}) collective-permute-start(bf16[64,1024]{1,0:T(8,128)(2,1)S(1)} %slice.304), channel_id=1, source_target_pairs={{0,1},{1,0},{2,3},{3,2},{4,5},{5,4},{6,7},{7,6},{8,10},{9,11},{10,... | collective-permute-start | bytes 393224 | tf_op jit(solution)/shard_map/cond/branch_1_fun/ppermute | solution.py:38
  62.8 12.6 %collective-permute-start.48 = (bf16[256,768]{1,0:T(8,128)(2,1)S(1)}, bf16[256,768]{1,0:T(8,128)(2,1)S(1)}, u32[]{:S(2)}, u32[]{:S(2)}) collective-permute-start(bf16[256,768]{1,0:T(8,128)(2,1)S(1)} %slice.300), channel_id=1, source_target_pairs={{0,2},{1,3},{2,0},{3,1},{4,6},{5,7},{6,4},{7,5},{8,9},{9,8},{10,11... | collective-permute-start | bytes 1179656 | tf_op jit(solution)/shard_map/cond/branch_1_fun/ppermute | solution.py:38
  68.7 6.0 %collective-permute-start.59 = (bf16[32,1024]{1,0:T(8,128)(2,1)S(1)}, bf16[32,1024]{1,0:T(8,128)(2,1)S(1)}, u32[]{:S(2)}, u32[]{:S(2)}) collective-permute-start(bf16[32,1024]{1,0:T(8,128)(2,1)S(1)} %slice.307), channel_id=1, source_target_pairs={{0,4},{1,5},{2,6},{3,7},{4,0},{5,1},{6,2},{7,3},{8,12},{9,13},{10,... | collective-permute-start | bytes 196616 | tf_op jit(solution)/shard_map/cond/branch_1_fun/ppermute | solution.py:38
  69.4 12.2 %collective-permute-start.51 = (bf16[256,768]{1,0:T(8,128)(2,1)S(1)}, bf16[256,768]{1,0:T(8,128)(2,1)S(1)}, u32[]{:S(2)}, u32[]{:S(2)}) collective-permute-start(bf16[256,768]{1,0:T(8,128)(2,1)S(1)} %slice.299), channel_id=1, source_target_pairs={{0,2},{1,3},{2,0},{3,1},{4,6},{5,7},{6,4},{7,5},{8,9},{9,8},{10,11... | collective-permute-start | bytes 1179656 | tf_op jit(solution)/shard_map/cond/branch_1_fun/ppermute | solution.py:38
  75.5 8.3 %collective-permute-start.53 = (bf16[128,768]{1,0:T(8,128)(2,1)S(1)}, bf16[128,768]{1,0:T(8,128)(2,1)S(1)}, u32[]{:S(2)}, u32[]{:S(2)}) collective-permute-start(bf16[128,768]{1,0:T(8,128)(2,1)S(1)} %slice.303), channel_id=1, source_target_pairs={{0,1},{1,0},{2,3},{3,2},{4,5},{5,4},{6,7},{7,6},{8,10},{9,11},{10,... | collective-permute-start | bytes 589832 | tf_op jit(solution)/shard_map/cond/branch_1_fun/ppermute | solution.py:38
  81.7 6.8 %collective-permute-start.55 = (bf16[128,768]{1,0:T(8,128)(2,1)S(1)}, bf16[128,768]{1,0:T(8,128)(2,1)S(1)}, u32[]{:S(2)}, u32[]{:S(2)}) collective-permute-start(bf16[128,768]{1,0:T(8,128)(2,1)S(1)} %slice.302), channel_id=1, source_target_pairs={{0,1},{1,0},{2,3},{3,2},{4,5},{5,4},{6,7},{7,6},{8,10},{9,11},{10,... | collective-permute-start | bytes 589832 | tf_op jit(solution)/shard_map/cond/branch_1_fun/ppermute | solution.py:38
  83.5 9.2 %collective-permute-start.52 = (bf16[128,1024]{1,0:T(8,128)(2,1)S(1)}, bf16[128,1024]{1,0:T(8,128)(2,1)S(1)}, u32[]{:S(2)}, u32[]{:S(2)}) collective-permute-start(bf16[128,1024]{1,0:T(8,128)(2,1)S(1)} %slice.238), channel_id=1, source_target_pairs={{7,0},{0,1},{1,2},{2,3},{3,4},{4,5},{5,6},{6,7},{15,8},{8,9},{9,10... | collective-permute-start | bytes 786440 | tf_op jit(solution)/shard_map/cond/branch_1_fun/ppermute | solution.py:46
  83.9 9.8 %collective-permute-start.54 = (bf16[64,768]{1,0:T(8,128)(2,1)S(1)}, bf16[64,768]{1,0:T(8,128)(2,1)S(1)}, u32[]{:S(2)}, u32[]{:S(2)}) collective-permute-start(bf16[64,768]{1,0:T(8,128)(2,1)S(1)} %slice.306), channel_id=1, source_target_pairs={{0,4},{1,5},{2,6},{3,7},{4,0},{5,1},{6,2},{7,3},{8,12},{9,13},{10,... | collective-permute-start | bytes 294920 | tf_op jit(solution)/shard_map/cond/branch_1_fun/ppermute | solution.py:38
  88.6 5.6 %collective-permute-start.56 = (bf16[64,768]{1,0:T(8,128)(2,1)S(1)}, bf16[64,768]{1,0:T(8,128)(2,1)S(1)}, u32[]{:S(2)}, u32[]{:S(2)}) collective-permute-start(bf16[64,768]{1,0:T(8,128)(2,1)S(1)} %slice.305), channel_id=1, source_target_pairs={{0,4},{1,5},{2,6},{3,7},{4,0},{5,1},{6,2},{7,3},{8,12},{9,13},{10,... | collective-permute-start | bytes 294920 | tf_op jit(solution)/shard_map/cond/branch_1_fun/ppermute | solution.py:38
  (4 other events, 32.4 us)

commit v3 on v2

--- a/solution.py
+++ b/solution.py
@@ -366,7 +366,7 @@
         moved=6 << 20,
         name="bwd_b",
     )(packed, attn, after(gctx, swapped_out), ordered)
-    swapped_b = swap_cores(send_b)
+    swapped_b = swap_cores(after(send_b, swapped_a))
     kept_out, last_out, _, _ = scatter_from(keep_out, swapped_out, rows)
     grad_out = kept_out + last_out.astype(F32)
     kept_a, last_a, first_a, seen_a = scatter_from(keep_a, swapped_a, rows)

time: 96.7 us -> 96.6 us (level)
  no operation moved by 1% of the time
where the time goes in v3:
time: 96.6 us; the launch traced here: 94.9 us
  waiting for transfers between devices  40.7 us (42%)
  starting transfers between devices  26.8 us (28%)
  Pallas kernels  14.6 us (15%)
  other arithmetic  7.01 us (7%)
  local copies, waits for them, and re-layouts  3.84 us (4%)
  between operations  1.28 us (1%)
    ppermute x16, waiting for transfers between devices, exchange(): return lax.ppermute(block, ('fsdp', 'rows'), pairs)  35.2 us
    ppermute x16, starting transfers between devices, exchange(): return lax.ppermute(block, ('fsdp', 'rows'), pairs)  23.2 us
    ppermute x3, waiting for transfers between devices, shifted(): lax.ppermute(block, 'rows', [((i - distance) % rows, i) for i in range(ro...  5.45 us
    pallas_call x1, Pallas kernels, branch(): call(functools.partial(forward_kernel, blocks=blocks), [((dim, 3 * hidden...  3.2 us
    pallas_call x1, Pallas kernels, branch(): call(backward_a_kernel, [((cells, hidden), BF16)] + half_outs, [VM] * 5,...  2.62 us
    ppermute x11, starting transfers between devices, swap_cores(): return lax.ppermute(block, 'fsdp', [(0, 1), (1, 0)])  2.23 us
    pallas_call x1, Pallas kernels, branch(): call(backward_b_kernel, half_outs, [VM, VM, VM, VM], flops=4 * cells * di...  2.21 us
    slice x5, local copies, waits for them, and re-layouts, branch(): part = lambda a: lax.slice_in_dim(a, low, low + half, axis=0)  1.97 us
  transfers between devices with their start and end apart: 30, of which 13 were waited for; matrix products, arithmetic and copies ran while one was open for 10% of the time, Pallas kernels for 10%

profile of v3, /device:TPU:0, one launch (start us, length us, event | category | flops | bytes accessed | tf_op | source)
XLA Modules:
  0.0 94.9 jit_solution(11260604663746715456)
XLA Ops:
  1.3 93.6 %conditional.1 = (bf16[1,16,16,1024]{3,2,1,0:T(8,128)(2,1)}, bf16[1,16,16,1024]{3,2,1,0:T(8,128)(2,1)}, f32[64,1536]{1,0:T(8,128)}, f32[32,1024]{1,0:T(8,128)}) conditional(s32[]{:T(128)} %bitcast.18, (bf16[1,16,16,1024]{3,2,1,0:T(8,128)(2,1)}, s32[8]{0:T(128)}, s32[8]{0:T(128)}, s32[1,16,16]{2,1,0:T(8,128)}, bf16[1,16,16,1024]{3,2,1,0:T(8,128)(2,1)}, ...), branch_computations={%region_0.1_spmd, %region_1.2_spmd} | conditional | flops 6992472064 | bytes 108641328 | solution.py:406
  3.3 4.1 %collective-permute-start.31 = (bf16[64,2048]{1,0:T(8,128)(2,1)S(1)}, bf16[64,2048]{1,0:T(8,128)(2,1)S(1)}, u32[]{:S(2)}, u32[]{:S(2)}) collective-permute-start(bf16[64,2048]{1,0:T(8,128)(2,1)S(1)} %maximum_maximum_fusion.1.refs_0_), channel_id=1, source_target_pairs={{0,4},{1,5},{2,6},{3,7},{4,0},{5,1},{6,2},{7,3},{8,12},{9,13},{10,... | collective-permute-start | bytes 786440 | tf_op jit(solution)/shard_map/cond/branch_1_fun/ppermute | solution.py:38
  7.4 1.5 %collective-permute-start.32 = (bf16[64,2048]{1,0:T(8,128)(2,1)S(1)}, bf16[64,2048]{1,0:T(8,128)(2,1)S(1)}, u32[]{:S(2)}, u32[]{:S(2)}) collective-permute-start(bf16[64,2048]{1,0:T(8,128)(2,1)S(1)} %maximum_maximum_fusion.1.refs_0_), channel_id=1, source_target_pairs={{0,1},{1,0},{2,3},{3,2},{4,5},{5,4},{6,7},{7,6},{8,10},{9,11},{10,... | collective-permute-start | bytes 786440 | tf_op jit(solution)/shard_map/cond/branch_1_fun/ppermute | solution.py:38
  8.9 1.6 %collective-permute-start.34 = (bf16[64,2048]{1,0:T(8,128)(2,1)S(1)}, bf16[64,2048]{1,0:T(8,128)(2,1)S(1)}, u32[]{:S(2)}, u32[]{:S(2)}) collective-permute-start(bf16[64,2048]{1,0:T(8,128)(2,1)S(1)} %maximum_maximum_fusion.1.refs_0_), channel_id=1, source_target_pairs={{0,2},{1,3},{2,0},{3,1},{4,6},{5,7},{6,4},{7,5},{8,9},{9,8},{10,11... | collective-permute-start | bytes 786440 | tf_op jit(solution)/shard_map/cond/branch_1_fun/ppermute | solution.py:38
  11.5 1.0 %slice.182 = bf16[1,8,16,1024]{3,2,1,0:T(8,128)(2,1)S(1)} slice(bf16[1,16,16,1024]{3,2,1,0:T(8,128)(2,1)} %get-tuple-element.76), slice={[0:1], [0:8], [0:16], [0:1024]} | slice | bytes 524288 | tf_op jit(solution)/shard_map/cond/branch_1_fun/slice | solution.py:293
  14.0 6.2 %collective-permute-done.31.refs_1_ = bf16[64,2048]{1,0:T(8,128)(2,1)S(1)} collective-permute-done((bf16[64,2048]{1,0:T(8,128)(2,1)S(1)}, bf16[64,2048]{1,0:T(8,128)(2,1)S(1)}, u32[]{:S(2)}, u32[]{:S(2)}) %collective-permute-start.31) | collective-permute-done | bytes 262176 | tf_op jit(solution)/shard_map/cond/branch_1_fun/ppermute | solution.py:38
  21.0 1.2 %collective-permute-start.35 = (bf16[64,2048]{1,0:T(8,128)(2,1)S(1)}, bf16[64,2048]{1,0:T(8,128)(2,1)S(1)}, u32[]{:S(2)}, u32[]{:S(2)}) collective-permute-start(bf16[64,2048]{1,0:T(8,128)(2,1)S(1)} %collective-permute-done.31.refs_1_), channel_id=1, source_target_pairs={{0,2},{1,3},{2,0},{3,1},{4,6},{5,7},{6,4},{7,5},{8,9},{9,8},{10,11... | collective-permute-start | bytes 786440 | tf_op jit(solution)/shard_map/cond/branch_1_fun/ppermute | solution.py:38
  22.3 1.3 %fusion.23 = s32[256]{0:T(256)S(1)} fusion(pred[]{:T(512)S(6)} %eq.45, s32[]{:T(128)} %bitcast.13, s32[]{:T(128)} %bitcast.12), kind=kLoop, calls=%fused_computation.92 | loop fusion | flops 4608 | bytes 1033 | tf_op jit(solution)/shard_map/cond/branch_1_fun/add | solution.py:313
  24.5 11.9 %collective-permute-done.33.refs_3_ = bf16[64,2048]{1,0:T(8,128)(2,1)S(1)} collective-permute-done((bf16[64,2048]{1,0:T(8,128)(2,1)S(1)}, bf16[64,2048]{1,0:T(8,128)(2,1)S(1)}, u32[]{:S(2)}, u32[]{:S(2)}) %collective-permute-start.33) | collective-permute-done | bytes 262176 | tf_op jit(solution)/shard_map/cond/branch_1_fun/ppermute | solution.py:38
  37.4 1.3 %collective-permute-start.37 = (bf16[64,2048]{1,0:T(8,128)(2,1)S(1)}, bf16[64,2048]{1,0:T(8,128)(2,1)S(1)}, u32[]{:S(2)}, u32[]{:S(2)}) collective-permute-start(bf16[64,2048]{1,0:T(8,128)(2,1)S(1)} %collective-permute-done.33.refs_3_), channel_id=1, source_target_pairs={{0,2},{1,3},{2,0},{3,1},{4,6},{5,7},{6,4},{7,5},{8,9},{9,8},{10,11... | collective-permute-start | bytes 786440 | tf_op jit(solution)/shard_map/cond/branch_1_fun/ppermute | solution.py:38
  40.8 3.0 %collective-permute-done.37.refs_7_ = bf16[64,2048]{1,0:T(8,128)(2,1)S(1)} collective-permute-done((bf16[64,2048]{1,0:T(8,128)(2,1)S(1)}, bf16[64,2048]{1,0:T(8,128)(2,1)S(1)}, u32[]{:S(2)}, u32[]{:S(2)}) %collective-permute-start.37) | collective-permute-done | bytes 262176 | tf_op jit(solution)/shard_map/cond/branch_1_fun/ppermute | solution.py:38
  44.4 1.7 %norm.3 = (bf16[256,1024]{1,0:T(8,128)(2,1)S(1)}, bf16[256,1024]{1,0:T(8,128)(2,1)S(1)}, bf16[1024,256]{1,0:T(8,128)(2,1)S(1)}, f32[256,1]{1,0:T(8,128)S(1)}, f32[256,1]{1,0:T(8,128)S(1)}) custom-call(s32[2]{0:T(128)S(1)} %copy-done.5, s32[16]{0:T(128)S(1)} %pad_add_fusion.1.table.place_at.order, bf16[256,1024]{1,0:T(8,128)(2,1)} %bitcast.24, ...), custom_call_target="tpu_custom_call" | custom-call | flops 5242880 | bytes 2621440 | tf_op jit(solution)/shard_map/cond/branch_1_fun/norm/pallas_call | solution.py:322
  46.3 3.2 %fwd.3 = (bf16[1024,1536]{1,0:T(8,128)(2,1)S(1)}, bf16[512,1024]{1,0:T(8,128)(2,1)S(1)}, bf16[256,1536]{1,0:T(8,128)(2,1)S(1)}, f32[8,256,256]{2,1,0:T(8,128)S(1...) custom-call(s32[16]{0:T(128)S(1)} %pad_add_fusion.1.table.place_at.order, ...), custom_call_target="tpu_custom_call" | custom-call | flops 2415919104 | bytes 10485760 | tf_op jit(solution)/shard_map/cond/branch_1_fun/fwd/pallas_call | solution.py:331
  49.5 1.0 %term_out.3 = (bf16[256,1024]{1,0:T(8,128)(2,1)S(1)}, f32[256,1024]{1,0:T(8,128)S(1)}, bf16[256,1024]{1,0:T(8,128)(2,1)S(1)}) custom-call(s32[2]{0:T(128)S(1)} %copy-done.5, bf16[512,256]{1,0:T(8,128)(2,1)S(1)} %get-tuple-element.85.ctx_ordered, bf16[256,1024]{1,0:T(8,128)(2,1)S(1)} %bitcast.27, bf16[128,1024]{1,0:T(8,128)(2,1)S(1)} %slice.236.halo), custom_call_target="tpu_custom_call" | custom-call | flops 268435456 | bytes 4194304 | tf_op jit(solution)/shard_map/cond/branch_1_fun/term_out/pallas_call | solution.py:340
  51.1 2.6 %bwd_a.3 = (bf16[256,512]{1,0:T(8,128)(2,1)S(1)}, bf16[256,768]{1,0:T(8,128)(2,1)S(1)}, f32[512,768]{1,0:T(8,128)S(1)}, bf16[512,768]{1,0:T(8,128)(2,1)S(1)}) custom-call(bf16[256,1024]{1,0:T(8,128)(2,1)S(1)} %get-tuple-element.86.cot, bf16[256,1536]{1,0:T(8,128)(2,1)S(1)} %get-tuple-element.87.packed, f32[8,256,256]{2,1,0:T(8,128)S(1)} %get-tuple-element.88.attn, ...), custom_call_target="tpu_custom_call" | custom-call | flops 1610612736 | bytes 6291456 | tf_op jit(solution)/shard_map/cond/branch_1_fun/bwd_a/pallas_call | solution.py:351
  54.1 1.4 %collective-permute-start.57 = (bf16[128,1024]{1,0:T(8,128)(2,1)S(1)}, bf16[128,1024]{1,0:T(8,128)(2,1)S(1)}, u32[]{:S(2)}, u32[]{:S(2)}) collective-permute-start(bf16[128,1024]{1,0:T(8,128)(2,1)S(1)} %slice.301), channel_id=1, source_target_pairs={{0,2},{1,3},{2,0},{3,1},{4,6},{5,7},{6,4},{7,5},{8,9},{9,8},{10,11... | collective-permute-start | bytes 786440 | tf_op jit(solution)/shard_map/cond/branch_1_fun/ppermute | solution.py:38
  56.1 1.2 %collective-permute-start.46 = (bf16[128,512]{1,0:T(8,128)(2,1)S(1)}, bf16[128,512]{1,0:T(8,128)(2,1)S(1)}, u32[]{:S(2)}, u32[]{:S(2)}) collective-permute-start(bf16[128,512]{1,0:T(8,128)(2,1)S(1)} %slice.189), channel_id=1, source_target_pairs={{7,0},{0,1},{1,2},{2,3},{3,4},{4,5},{5,6},{6,7},{15,8},{8,9},{9,10... | collective-permute-start | bytes 393224 | tf_op jit(solution)/shard_map/cond/branch_1_fun/ppermute | solution.py:46
  57.3 2.2 %bwd_b.3 = (bf16[256,768]{1,0:T(8,128)(2,1)S(1)}, f32[512,768]{1,0:T(8,128)S(1)}, bf16[512,768]{1,0:T(8,128)(2,1)S(1)}) custom-call(bf16[256,1536]{1,0:T(8,128)(2,1)S(1)} %get-tuple-element.87.packed, f32[8,256,256]{2,1,0:T(8,128)S(1)} %get-tuple-element.88.attn, bf16[256,512]{1,0:T(8,128)(2,1)S(1)} %get-tuple-element.101.gctx, ...), custom_call_target="tpu_custom_call" | custom-call | flops 1610612736 | bytes 6291456 | tf_op jit(solution)/shard_map/cond/branch_1_fun/bwd_b/pallas_call | solution.py:361
  60.6 2.0 %collective-permute-start.58 = (bf16[64,1024]{1,0:T(8,128)(2,1)S(1)}, bf16[64,1024]{1,0:T(8,128)(2,1)S(1)}, u32[]{:S(2)}, u32[]{:S(2)}) collective-permute-start(bf16[64,1024]{1,0:T(8,128)(2,1)S(1)} %slice.304), channel_id=1, source_target_pairs={{0,1},{1,0},{2,3},{3,2},{4,5},{5,4},{6,7},{7,6},{8,10},{9,11},{10,... | collective-permute-start | bytes 393224 | tf_op jit(solution)/shard_map/cond/branch_1_fun/ppermute | solution.py:38
  62.8 1.3 %collective-permute-start.48 = (bf16[256,768]{1,0:T(8,128)(2,1)S(1)}, bf16[256,768]{1,0:T(8,128)(2,1)S(1)}, u32[]{:S(2)}, u32[]{:S(2)}) collective-permute-start(bf16[256,768]{1,0:T(8,128)(2,1)S(1)} %slice.300), channel_id=1, source_target_pairs={{0,2},{1,3},{2,0},{3,1},{4,6},{5,7},{6,4},{7,5},{8,9},{9,8},{10,11... | collective-permute-start | bytes 1179656 | tf_op jit(solution)/shard_map/cond/branch_1_fun/ppermute | solution.py:38
  64.2 1.8 %collective-permute-done.46.back = bf16[128,512]{1,0:T(8,128)(2,1)S(1)} collective-permute-done((bf16[128,512]{1,0:T(8,128)(2,1)S(1)}, bf16[128,512]{1,0:T(8,128)(2,1)S(1)}, u32[]{:S(2)}, u32[]{:S(2)}) %collective-permute-start.46) | collective-permute-done | bytes 131104 | tf_op jit(solution)/shard_map/cond/branch_1_fun/ppermute | solution.py:46
  66.0 1.3 %grad.3 = bf16[256,1024]{1,0:T(8,128)(2,1)S(1)} custom-call(bf16[256,1024]{1,0:T(8,128)(2,1)S(1)} %get-tuple-element.96.xw, f32[256,1]{1,0:T(8,128)S(1)} %get-tuple-element.97.mean, f32[256,1]{1,0:T(8,128)S(1)} %get-tuple-element.98.inv, bf16[256,768]{1,0:T(8,128)(2,1)S(1)} %get-tuple-element.91.gp_a, bf16[256,768]{1,0:T(8,128)(2,1)S(1)} %get-tuple-element.103.gp_b, ...), custom_call_target="tpu_custom_call" | custom-call | flops 805306368 | bytes 6291456 | tf_op jit(solution)/shard_map/cond/branch_1_fun/grad/pallas_call | solution.py:381
  67.3 1.3 %collective-permute-done.58 = bf16[64,1024]{1,0:T(8,128)(2,1)S(1)} collective-permute-done((bf16[64,1024]{1,0:T(8,128)(2,1)S(1)}, bf16[64,1024]{1,0:T(8,128)(2,1)S(1)}, u32[]{:S(2)}, u32[]{:S(2)}) %collective-permute-start.58) | collective-permute-done | bytes 131104 | tf_op jit(solution)/shard_map/cond/branch_1_fun/ppermute | solution.py:38
  69.4 2.8 %collective-permute-start.51 = (bf16[256,768]{1,0:T(8,128)(2,1)S(1)}, bf16[256,768]{1,0:T(8,128)(2,1)S(1)}, u32[]{:S(2)}, u32[]{:S(2)}) collective-permute-start(bf16[256,768]{1,0:T(8,128)(2,1)S(1)} %slice.299), channel_id=1, source_target_pairs={{0,2},{1,3},{2,0},{3,1},{4,6},{5,7},{6,4},{7,5},{8,9},{9,8},{10,11... | collective-permute-start | bytes 1179656 | tf_op jit(solution)/shard_map/cond/branch_1_fun/ppermute | solution.py:38
  72.1 2.6 %collective-permute-done.59 = bf16[32,1024]{1,0:T(8,128)(2,1)S(1)} collective-permute-done((bf16[32,1024]{1,0:T(8,128)(2,1)S(1)}, bf16[32,1024]{1,0:T(8,128)(2,1)S(1)}, u32[]{:S(2)}, u32[]{:S(2)}) %collective-permute-start.59) | collective-permute-done | bytes 65568 | tf_op jit(solution)/shard_map/cond/branch_1_fun/ppermute | solution.py:38
  75.6 1.8 %output.3 = bf16[256,1024]{1,0:T(8,128)(2,1)} custom-call(s32[2]{0:T(128)S(1)} %copy-done.5, bf16[256,1024]{1,0:T(8,128)(2,1)S(1)} %bitcast.25, bf16[256,512]{1,0:T(8,128)(2,1)S(1)} %get-tuple-element.84.ctx, bf16[128,512]{1,0:T(8,128)(2,1)S(1)} %collective-permute-done.46.back, bf16[512,1024]{1,0:T(8,128)(2,1)S(1)} %get-tuple-element.90.full), custom_call_target="tpu_custom_call" | custom-call | flops 268435456 | bytes 3145728 | tf_op jit(solution)/shard_map/cond/branch_1_fun/output/pallas_call | solution.py:391
  77.4 4.2 %collective-permute-done.51 = bf16[256,768]{1,0:T(8,128)(2,1)S(1)} collective-permute-done((bf16[256,768]{1,0:T(8,128)(2,1)S(1)}, bf16[256,768]{1,0:T(8,128)(2,1)S(1)}, u32[]{:S(2)}, u32[]{:S(2)}) %collective-permute-start.51) | collective-permute-done | bytes 393248 | tf_op jit(solution)/shard_map/cond/branch_1_fun/ppermute | solution.py:38
  81.7 1.8 %collective-permute-start.55 = (bf16[128,768]{1,0:T(8,128)(2,1)S(1)}, bf16[128,768]{1,0:T(8,128)(2,1)S(1)}, u32[]{:S(2)}, u32[]{:S(2)}) collective-permute-start(bf16[128,768]{1,0:T(8,128)(2,1)S(1)} %slice.302), channel_id=1, source_target_pairs={{0,1},{1,0},{2,3},{3,2},{4,5},{5,4},{6,7},{7,6},{8,10},{9,11},{10,... | collective-permute-start | bytes 589832 | tf_op jit(solution)/shard_map/cond/branch_1_fun/ppermute | solution.py:38
  83.9 1.3 %collective-permute-start.54 = (bf16[64,768]{1,0:T(8,128)(2,1)S(1)}, bf16[64,768]{1,0:T(8,128)(2,1)S(1)}, u32[]{:S(2)}, u32[]{:S(2)}) collective-permute-start(bf16[64,768]{1,0:T(8,128)(2,1)S(1)} %slice.306), channel_id=1, source_target_pairs={{0,4},{1,5},{2,6},{3,7},{4,0},{5,1},{6,2},{7,3},{8,12},{9,13},{10,... | collective-permute-start | bytes 294920 | tf_op jit(solution)/shard_map/cond/branch_1_fun/ppermute | solution.py:38
  85.2 3.3 %collective-permute-done.55 = bf16[128,768]{1,0:T(8,128)(2,1)S(1)} collective-permute-done((bf16[128,768]{1,0:T(8,128)(2,1)S(1)}, bf16[128,768]{1,0:T(8,128)(2,1)S(1)}, u32[]{:S(2)}, u32[]{:S(2)}) %collective-permute-start.55) | collective-permute-done | bytes 196640 | tf_op jit(solution)/shard_map/cond/branch_1_fun/ppermute | solution.py:38
  89.1 3.6 %collective-permute-done.52 = bf16[128,1024]{1,0:T(8,128)(2,1)S(1)} collective-permute-done((bf16[128,1024]{1,0:T(8,128)(2,1)S(1)}, bf16[128,1024]{1,0:T(8,128)(2,1)S(1)}, u32[]{:S(2)}, u32[]{:S(2)}) %collective-permute-start.52) | collective-permute-done | bytes 262176 | tf_op jit(solution)/shard_map/cond/branch_1_fun/ppermute | solution.py:46
  92.7 1.0 %pad_select_fusion.1 = bf16[256,1024]{1,0:T(8,128)(2,1)} fusion(bf16[256,1024]{1,0:T(8,128)(2,1)S(1)} %grad.3, bf16[128,1024]{1,0:T(8,128)(2,1)S(1)} %collective-permute-done.52, pred[256]{0:T(512)(128)(4,1)S(1)} %fusion.24), kind=kLoop, calls=%fused_computation.67 | loop fusion | flops 262144 | bytes 1310976 | tf_op jit(solution)/shard_map/cond/branch_1_fun/jit(_where)/select_n | solution.py:400
  (92 shorter events, 16.3 us)
Async XLA Ops:
  1.5 22.0 %copy-start.9 = (s32[8]{0:T(128)S(1)}, s32[8]{0:T(128)}, u32[]{:S(2)}) copy-start(s32[8]{0:T(128)} %get-tuple-element.73) | copy-start | bytes 100 | tf_op jit(solution)/shard_map/cond
  1.6 22.0 %copy-start.11 = (s32[8]{0:T(128)S(1)}, s32[8]{0:T(128)}, u32[]{:S(2)}) copy-start(s32[8]{0:T(128)} %get-tuple-element.74) | copy-start | bytes 100 | tf_op jit(solution)/shard_map/cond
  3.3 16.9 %collective-permute-start.31 = (bf16[64,2048]{1,0:T(8,128)(2,1)S(1)}, bf16[64,2048]{1,0:T(8,128)(2,1)S(1)}, u32[]{:S(2)}, u32[]{:S(2)}) collective-permute-start(bf16[64,2048]{1,0:T(8,128)(2,1)S(1)} %maximum_maximum_fusion.1.refs_0_), channel_id=1, source_target_pairs={{0,4},{1,5},{2,6},{3,7},{4,0},{5,1},{6,2},{7,3},{8,12},{9,13},{10,... | collective-permute-start | bytes 786440 | tf_op jit(solution)/shard_map/cond/branch_1_fun/ppermute | solution.py:38
  7.4 12.8 %collective-permute-start.32 = (bf16[64,2048]{1,0:T(8,128)(2,1)S(1)}, bf16[64,2048]{1,0:T(8,128)(2,1)S(1)}, u32[]{:S(2)}, u32[]{:S(2)}) collective-permute-start(bf16[64,2048]{1,0:T(8,128)(2,1)S(1)} %maximum_maximum_fusion.1.refs_0_), channel_id=1, source_target_pairs={{0,1},{1,0},{2,3},{3,2},{4,5},{5,4},{6,7},{7,6},{8,10},{9,11},{10,... | collective-permute-start | bytes 786440 | tf_op jit(solution)/shard_map/cond/branch_1_fun/ppermute | solution.py:38
  8.9 12.1 %collective-permute-start.34 = (bf16[64,2048]{1,0:T(8,128)(2,1)S(1)}, bf16[64,2048]{1,0:T(8,128)(2,1)S(1)}, u32[]{:S(2)}, u32[]{:S(2)}) collective-permute-start(bf16[64,2048]{1,0:T(8,128)(2,1)S(1)} %maximum_maximum_fusion.1.refs_0_), channel_id=1, source_target_pairs={{0,2},{1,3},{2,0},{3,1},{4,6},{5,7},{6,4},{7,5},{8,9},{9,8},{10,11... | collective-permute-start | bytes 786440 | tf_op jit(solution)/shard_map/cond/branch_1_fun/ppermute | solution.py:38
  13.4 23.9 %collective-permute-start.30 = (bf16[272,1024]{1,0:T(8,128)(2,1)}, bf16[272,1024]{1,0:T(8,128)(2,1)S(1)}, u32[]{:S(2)}, u32[]{:S(2)}) collective-permute-start(bf16[272,1024]{1,0:T(8,128)(2,1)} %fusion.17), channel_id=1, source_target_pairs={{1,0},{2,1},{3,2},{4,3},{5,4},{6,5},{7,6},{0,7},{9,8},{10,9},{11,1... | collective-permute-start | bytes 1671176 | tf_op jit(solution)/shard_map/cond/branch_1_fun/ppermute | solution.py:46
  13.4 25.4 %collective-permute-start.38 = (bf16[64,2048]{1,0:T(8,128)(2,1)S(1)}, bf16[64,2048]{1,0:T(8,128)(2,1)S(1)}, u32[]{:S(2)}, u32[]{:S(2)}) collective-permute-start(bf16[64,2048]{1,0:T(8,128)(2,1)S(1)} %maximum_maximum_fusion.1.refs_0_), channel_id=1, source_target_pairs={{0,8},{8,0},{1,9},{9,1},{2,10},{10,2},{3,11},{11,3},{4,12},{12,4},... | collective-permute-start | bytes 786440 | tf_op jit(solution)/shard_map/cond/branch_1_fun/ppermute | solution.py:42
  20.2 16.1 %collective-permute-start.33 = (bf16[64,2048]{1,0:T(8,128)(2,1)S(1)}, bf16[64,2048]{1,0:T(8,128)(2,1)S(1)}, u32[]{:S(2)}, u32[]{:S(2)}) collective-permute-start(bf16[64,2048]{1,0:T(8,128)(2,1)S(1)} %collective-permute-done.31.refs_1_), channel_id=1, source_target_pairs={{0,1},{1,0},{2,3},{3,2},{4,5},{5,4},{6,7},{7,6},{8,10},{9,11},{10,... | collective-permute-start | bytes 786440 | tf_op jit(solution)/shard_map/cond/branch_1_fun/ppermute | solution.py:38
  21.0 16.3 %collective-permute-start.35 = (bf16[64,2048]{1,0:T(8,128)(2,1)S(1)}, bf16[64,2048]{1,0:T(8,128)(2,1)S(1)}, u32[]{:S(2)}, u32[]{:S(2)}) collective-permute-start(bf16[64,2048]{1,0:T(8,128)(2,1)S(1)} %collective-permute-done.31.refs_1_), channel_id=1, source_target_pairs={{0,2},{1,3},{2,0},{3,1},{4,6},{5,7},{6,4},{7,5},{8,9},{9,8},{10,11... | collective-permute-start | bytes 786440 | tf_op jit(solution)/shard_map/cond/branch_1_fun/ppermute | solution.py:38
  23.6 16.6 %collective-permute-start.36 = (bf16[64,2048]{1,0:T(8,128)(2,1)S(1)}, bf16[64,2048]{1,0:T(8,128)(2,1)S(1)}, u32[]{:S(2)}, u32[]{:S(2)}) collective-permute-start(bf16[64,2048]{1,0:T(8,128)(2,1)S(1)} %collective-permute-done.32.refs_2_), channel_id=1, source_target_pairs={{0,2},{1,3},{2,0},{3,1},{4,6},{5,7},{6,4},{7,5},{8,9},{9,8},{10,11... | collective-permute-start | bytes 786440 | tf_op jit(solution)/shard_map/cond/branch_1_fun/ppermute | solution.py:38
  36.4 3.8 %collective-permute-start.39 = (bf16[64,2048]{1,0:T(8,128)(2,1)S(1)}, bf16[64,2048]{1,0:T(8,128)(2,1)S(1)}, u32[]{:S(2)}, u32[]{:S(2)}) collective-permute-start(bf16[64,2048]{1,0:T(8,128)(2,1)S(1)} %collective-permute-done.31.refs_1_), channel_id=1, source_target_pairs={{0,8},{8,0},{1,9},{9,1},{2,10},{10,2},{3,11},{11,3},{4,12},{12,4},... | collective-permute-start | bytes 786440 | tf_op jit(solution)/shard_map/cond/branch_1_fun/ppermute | solution.py:42
  37.4 3.3 %collective-permute-start.40 = (bf16[64,2048]{1,0:T(8,128)(2,1)S(1)}, bf16[64,2048]{1,0:T(8,128)(2,1)S(1)}, u32[]{:S(2)}, u32[]{:S(2)}) collective-permute-start(bf16[64,2048]{1,0:T(8,128)(2,1)S(1)} %collective-permute-done.32.refs_2_), channel_id=1, source_target_pairs={{0,8},{8,0},{1,9},{9,1},{2,10},{10,2},{3,11},{11,3},{4,12},{12,4},... | collective-permute-start | bytes 786440 | tf_op jit(solution)/shard_map/cond/branch_1_fun/ppermute | solution.py:42
  37.4 6.4 %collective-permute-start.37 = (bf16[64,2048]{1,0:T(8,128)(2,1)S(1)}, bf16[64,2048]{1,0:T(8,128)(2,1)S(1)}, u32[]{:S(2)}, u32[]{:S(2)}) collective-permute-start(bf16[64,2048]{1,0:T(8,128)(2,1)S(1)} %collective-permute-done.33.refs_3_), channel_id=1, source_target_pairs={{0,2},{1,3},{2,0},{3,1},{4,6},{5,7},{6,4},{7,5},{8,9},{9,8},{10,11... | collective-permute-start | bytes 786440 | tf_op jit(solution)/shard_map/cond/branch_1_fun/ppermute | solution.py:38
  38.9 7.4 %collective-permute-start.42 = (bf16[64,2048]{1,0:T(8,128)(2,1)S(1)}, bf16[64,2048]{1,0:T(8,128)(2,1)S(1)}, u32[]{:S(2)}, u32[]{:S(2)}) collective-permute-start(bf16[64,2048]{1,0:T(8,128)(2,1)S(1)} %collective-permute-done.34.refs_4_), channel_id=1, source_target_pairs={{0,8},{8,0},{1,9},{9,1},{2,10},{10,2},{3,11},{11,3},{4,12},{12,4},... | collective-permute-start | bytes 786440 | tf_op jit(solution)/shard_map/cond/branch_1_fun/ppermute | solution.py:42
  40.2 6.1 %collective-permute-start.41 = (bf16[64,2048]{1,0:T(8,128)(2,1)S(1)}, bf16[64,2048]{1,0:T(8,128)(2,1)S(1)}, u32[]{:S(2)}, u32[]{:S(2)}) collective-permute-start(bf16[64,2048]{1,0:T(8,128)(2,1)S(1)} %collective-permute-done.33.refs_3_), channel_id=1, source_target_pairs={{0,8},{8,0},{1,9},{9,1},{2,10},{10,2},{3,11},{11,3},{4,12},{12,4},... | collective-permute-start | bytes 786440 | tf_op jit(solution)/shard_map/cond/branch_1_fun/ppermute | solution.py:42
  40.2 6.1 %collective-permute-start.43 = (bf16[64,2048]{1,0:T(8,128)(2,1)S(1)}, bf16[64,2048]{1,0:T(8,128)(2,1)S(1)}, u32[]{:S(2)}, u32[]{:S(2)}) collective-permute-start(bf16[64,2048]{1,0:T(8,128)(2,1)S(1)} %collective-permute-done.35.refs_5_), channel_id=1, source_target_pairs={{0,8},{8,0},{1,9},{9,1},{2,10},{10,2},{3,11},{11,3},{4,12},{12,4},... | collective-permute-start | bytes 786440 | tf_op jit(solution)/shard_map/cond/branch_1_fun/ppermute | solution.py:42
  40.7 5.6 %collective-permute-start.44 = (bf16[64,2048]{1,0:T(8,128)(2,1)S(1)}, bf16[64,2048]{1,0:T(8,128)(2,1)S(1)}, u32[]{:S(2)}, u32[]{:S(2)}) collective-permute-start(bf16[64,2048]{1,0:T(8,128)(2,1)S(1)} %collective-permute-done.36.refs_6_), channel_id=1, source_target_pairs={{0,8},{8,0},{1,9},{9,1},{2,10},{10,2},{3,11},{11,3},{4,12},{12,4},... | collective-permute-start | bytes 786440 | tf_op jit(solution)/shard_map/cond/branch_1_fun/ppermute | solution.py:42
  43.7 2.6 %collective-permute-start.45 = (bf16[64,2048]{1,0:T(8,128)(2,1)S(1)}, bf16[64,2048]{1,0:T(8,128)(2,1)S(1)}, u32[]{:S(2)}, u32[]{:S(2)}) collective-permute-start(bf16[64,2048]{1,0:T(8,128)(2,1)S(1)} %collective-permute-done.37.refs_7_), channel_id=1, source_target_pairs={{0,8},{8,0},{1,9},{9,1},{2,10},{10,2},{3,11},{11,3},{4,12},{12,4},... | collective-permute-start | bytes 786440 | tf_op jit(solution)/shard_map/cond/branch_1_fun/ppermute | solution.py:42
  50.6 3.3 %collective-permute-start.49 = (bf16[256,1024]{1,0:T(8,128)(2,1)S(1)}, bf16[256,1024]{1,0:T(8,128)(2,1)S(1)}, u32[]{:S(2)}, u32[]{:S(2)}) collective-permute-start(bf16[256,1024]{1,0:T(8,128)(2,1)S(1)} %get-tuple-element.100), channel_id=1, source_target_pairs={{0,8},{8,0},{1,9},{9,1},{2,10},{10,2},{3,11},{11,3},{4,12},{12,4},... | collective-permute-start | bytes 1572872 | tf_op jit(solution)/shard_map/cond/branch_1_fun/ppermute | solution.py:42
  53.8 5.8 %collective-permute-start.47 = (bf16[512,768]{1,0:T(8,128)(2,1)S(1)}, bf16[512,768]{1,0:T(8,128)(2,1)S(1)}, u32[]{:S(2)}, u32[]{:S(2)}) collective-permute-start(bf16[512,768]{1,0:T(8,128)(2,1)S(1)} %get-tuple-element.94), channel_id=1, source_target_pairs={{0,8},{8,0},{1,9},{9,1},{2,10},{10,2},{3,11},{11,3},{4,12},{12,4},... | collective-permute-start | bytes 2359304 | tf_op jit(solution)/shard_map/cond/branch_1_fun/ppermute | solution.py:42
  54.1 6.4 %collective-permute-start.57 = (bf16[128,1024]{1,0:T(8,128)(2,1)S(1)}, bf16[128,1024]{1,0:T(8,128)(2,1)S(1)}, u32[]{:S(2)}, u32[]{:S(2)}) collective-permute-start(bf16[128,1024]{1,0:T(8,128)(2,1)S(1)} %slice.301), channel_id=1, source_target_pairs={{0,2},{1,3},{2,0},{3,1},{4,6},{5,7},{6,4},{7,5},{8,9},{9,8},{10,11... | collective-permute-start | bytes 786440 | tf_op jit(solution)/shard_map/cond/branch_1_fun/ppermute | solution.py:38
  56.1 9.9 %collective-permute-start.46 = (bf16[128,512]{1,0:T(8,128)(2,1)S(1)}, bf16[128,512]{1,0:T(8,128)(2,1)S(1)}, u32[]{:S(2)}, u32[]{:S(2)}) collective-permute-start(bf16[128,512]{1,0:T(8,128)(2,1)S(1)} %slice.189), channel_id=1, source_target_pairs={{7,0},{0,1},{1,2},{2,3},{3,4},{4,5},{5,6},{6,7},{15,8},{8,9},{9,10... | collective-permute-start | bytes 393224 | tf_op jit(solution)/shard_map/cond/branch_1_fun/ppermute | solution.py:46
  59.5 9.6 %collective-permute-start.50 = (bf16[512,768]{1,0:T(8,128)(2,1)S(1)}, bf16[512,768]{1,0:T(8,128)(2,1)S(1)}, u32[]{:S(2)}, u32[]{:S(2)}) collective-permute-start(bf16[512,768]{1,0:T(8,128)(2,1)S(1)} %get-tuple-element.107), channel_id=1, source_target_pairs={{0,8},{8,0},{1,9},{9,1},{2,10},{10,2},{3,11},{11,3},{4,12},{12,4},... | collective-permute-start | bytes 2359304 | tf_op jit(solution)/shard_map/cond/branch_1_fun/ppermute | solution.py:42
  60.6 8.1 %collective-permute-start.58 = (bf16[64,1024]{1,0:T(8,128)(2,1)S(1)}, bf16[64,1024]{1,0:T(8,128)(2,1)S(1)}, u32[]{:S(2)}, u32[]{:S(2)}) collective-permute-start(bf16[64,1024]{1,0:T(8,128)(2,1)S(1)} %slice.304), channel_id=1, source_target_pairs={{0,1},{1,0},{2,3},{3,2},{4,5},{5,4},{6,7},{7,6},{8,10},{9,11},{10,... | collective-permute-start | bytes 393224 | tf_op jit(solution)/shard_map/cond/branch_1_fun/ppermute | solution.py:38
  62.8 12.6 %collective-permute-start.48 = (bf16[256,768]{1,0:T(8,128)(2,1)S(1)}, bf16[256,768]{1,0:T(8,128)(2,1)S(1)}, u32[]{:S(2)}, u32[]{:S(2)}) collective-permute-start(bf16[256,768]{1,0:T(8,128)(2,1)S(1)} %slice.300), channel_id=1, source_target_pairs={{0,2},{1,3},{2,0},{3,1},{4,6},{5,7},{6,4},{7,5},{8,9},{9,8},{10,11... | collective-permute-start | bytes 1179656 | tf_op jit(solution)/shard_map/cond/branch_1_fun/ppermute | solution.py:38
  68.7 6.0 %collective-permute-start.59 = (bf16[32,1024]{1,0:T(8,128)(2,1)S(1)}, bf16[32,1024]{1,0:T(8,128)(2,1)S(1)}, u32[]{:S(2)}, u32[]{:S(2)}) collective-permute-start(bf16[32,1024]{1,0:T(8,128)(2,1)S(1)} %slice.307), channel_id=1, source_target_pairs={{0,4},{1,5},{2,6},{3,7},{4,0},{5,1},{6,2},{7,3},{8,12},{9,13},{10,... | collective-permute-start | bytes 196616 | tf_op jit(solution)/shard_map/cond/branch_1_fun/ppermute | solution.py:38
  69.4 12.2 %collective-permute-start.51 = (bf16[256,768]{1,0:T(8,128)(2,1)S(1)}, bf16[256,768]{1,0:T(8,128)(2,1)S(1)}, u32[]{:S(2)}, u32[]{:S(2)}) collective-permute-start(bf16[256,768]{1,0:T(8,128)(2,1)S(1)} %slice.299), channel_id=1, source_target_pairs={{0,2},{1,3},{2,0},{3,1},{4,6},{5,7},{6,4},{7,5},{8,9},{9,8},{10,11... | collective-permute-start | bytes 1179656 | tf_op jit(solution)/shard_map/cond/branch_1_fun/ppermute | solution.py:38
  75.5 8.3 %collective-permute-start.53 = (bf16[128,768]{1,0:T(8,128)(2,1)S(1)}, bf16[128,768]{1,0:T(8,128)(2,1)S(1)}, u32[]{:S(2)}, u32[]{:S(2)}) collective-permute-start(bf16[128,768]{1,0:T(8,128)(2,1)S(1)} %slice.303), channel_id=1, source_target_pairs={{0,1},{1,0},{2,3},{3,2},{4,5},{5,4},{6,7},{7,6},{8,10},{9,11},{10,... | collective-permute-start | bytes 589832 | tf_op jit(solution)/shard_map/cond/branch_1_fun/ppermute | solution.py:38
  81.7 6.8 %collective-permute-start.55 = (bf16[128,768]{1,0:T(8,128)(2,1)S(1)}, bf16[128,768]{1,0:T(8,128)(2,1)S(1)}, u32[]{:S(2)}, u32[]{:S(2)}) collective-permute-start(bf16[128,768]{1,0:T(8,128)(2,1)S(1)} %slice.302), channel_id=1, source_target_pairs={{0,1},{1,0},{2,3},{3,2},{4,5},{5,4},{6,7},{7,6},{8,10},{9,11},{10,... | collective-permute-start | bytes 589832 | tf_op jit(solution)/shard_map/cond/branch_1_fun/ppermute | solution.py:38
  83.5 9.2 %collective-permute-start.52 = (bf16[128,1024]{1,0:T(8,128)(2,1)S(1)}, bf16[128,1024]{1,0:T(8,128)(2,1)S(1)}, u32[]{:S(2)}, u32[]{:S(2)}) collective-permute-start(bf16[128,1024]{1,0:T(8,128)(2,1)S(1)} %slice.238), channel_id=1, source_target_pairs={{7,0},{0,1},{1,2},{2,3},{3,4},{4,5},{5,6},{6,7},{15,8},{8,9},{9,10... | collective-permute-start | bytes 786440 | tf_op jit(solution)/shard_map/cond/branch_1_fun/ppermute | solution.py:46
  83.9 9.8 %collective-permute-start.54 = (bf16[64,768]{1,0:T(8,128)(2,1)S(1)}, bf16[64,768]{1,0:T(8,128)(2,1)S(1)}, u32[]{:S(2)}, u32[]{:S(2)}) collective-permute-start(bf16[64,768]{1,0:T(8,128)(2,1)S(1)} %slice.306), channel_id=1, source_target_pairs={{0,4},{1,5},{2,6},{3,7},{4,0},{5,1},{6,2},{7,3},{8,12},{9,13},{10,... | collective-permute-start | bytes 294920 | tf_op jit(solution)/shard_map/cond/branch_1_fun/ppermute | solution.py:38
  88.6 5.6 %collective-permute-start.56 = (bf16[64,768]{1,0:T(8,128)(2,1)S(1)}, bf16[64,768]{1,0:T(8,128)(2,1)S(1)}, u32[]{:S(2)}, u32[]{:S(2)}) collective-permute-start(bf16[64,768]{1,0:T(8,128)(2,1)S(1)} %slice.305), channel_id=1, source_target_pairs={{0,4},{1,5},{2,6},{3,7},{4,0},{5,1},{6,2},{7,3},{8,12},{9,13},{10,... | collective-permute-start | bytes 294920 | tf_op jit(solution)/shard_map/cond/branch_1_fun/ppermute | solution.py:38
  (4 other events, 32.4 us)
